TPU v7x, 128 devices: a whole 4x4x4 slice. The times are simulated.
128 devices in a mesh: tile: 8 (over x_hi, z), src: 16 (over y, x_lo, core).
Axes of the slice: x: 4 (x_hi: 2, x_lo: 2; x = x_hi * 2 + x_lo), y: 4, z: 4, core: 2. Of those that a mesh axis runs over, the one named last changes fastest.
Arguments:
- permittivity: float32 [128, 16, 320], P(('tile', 'src')), may hold values from 1 to 2
- e_start: float32 [16, 3, 128, 16, 320], P('src', None, 'tile'), may hold values from -6 to 6
- h_start: float32 [16, 3, 128, 16, 320], P('src', None, 'tile'), may hold values from -6 to 6
- e_cotangent: float32 [16, 3, 128, 16, 320], P('src', None, 'tile'), may hold values from -6 to 6
- h_cotangent: float32 [16, 3, 128, 16, 320], P('src', None, 'tile'), may hold values from -6 to 6
Outputs:
- e_final: float32 [16, 3, 128, 16, 320], P('src', None, 'tile')
- gradient: float32 [128, 16, 320], P(('tile', 'src'))
All inputs are finite; a program needn't handle non-finite values.
Results may differ from a plain program's by a relative error of at most 0.00002.
Values sent between devices are 32-bit elements; how exact they have to be, the bound alone decides.
No kernel may reach another device: no remote copies, remote signals or barrier semaphores. Data moves between devices by JAX's collectives and lax.ppermute only.
A program may use at most 64 MiB of HBM per device.

v0:
```python
import jax
import jax.numpy as jnp
from jax import lax
from jax.experimental import pallas as pl
from jax.experimental.pallas import tpu as pltpu
from jax.sharding import PartitionSpec as P


STEPS = 6
courant = 0.57
NX, NY, NZ = 16, 16, 320
WIDE = 384
DEEP = 6
GHOST = 12
ALL = GHOST + NX + 12


F32 = jnp.float32


def plane_list(depth, upward):
    if upward and depth == STEPS:
        return [(2, 1, 0), (2, 2, 0)] + [(a, c, p) for p in range(NX - depth + 1, NX) for a in range(2) for c in range(3)]
    if upward:
        return [(a, c, p) for p in range(NX - depth, NX) for a in range(2) for c in range(3)]
    whole = [(a, c, p) for p in range(depth - 1) for a in range(2) for c in range(3)]
    return whole + [(0, 1, depth - 1), (0, 2, depth - 1)]


def first_half_step(e, h, p, c):
    if c == 1:
        x = e(0, p)
        ahead = jnp.concatenate([x[:, 1:], jnp.zeros((NY, 1), F32)], axis=1) - x
        return h(1, p) - courant * (ahead - (e(2, p + 1) - e(2, p)))
    x = e(0, p)
    ahead = jnp.concatenate([x[1:], jnp.zeros((1, NZ), F32)], axis=0) - x
    return h(2, p) - courant * ((e(1, p + 1) - e(1, p)) - ahead)


def pack_body(depth, e_hbm, h_hbm, up_ref, dn_ref, low_ref, high_ref, sem):
    def edges(upward):
        start, ref = (NX - depth, high_ref) if upward else (0, low_ref)
        return [
            pltpu.make_async_copy(x.at[0, :, pl.ds(start, depth)], ref.at[a], sem.at[2 * upward + a])
            for a, x in enumerate((e_hbm, h_hbm))
        ]

    copies = {upward: edges(upward) for upward in (True, False)}
    for upward in (True, False):
        for copy in copies[upward]:
            copy.start()
    for upward, out in ((True, up_ref), (False, dn_ref)):
        for copy in copies[upward]:
            copy.wait()
        ref, base = (high_ref, NX - depth) if upward else (low_ref, 0)
        at = lambda a: lambda c, p, a=a, ref=ref, base=base: ref[a, c, p - base]
        planes = plane_list(depth, upward)
        for k in range(len(planes) // 2):
            tails = []
            for j in range(2):
                a, c, p = planes[2 * k + j]
                x = first_half_step(at(0), at(1), NX - depth, c) if a == 2 else at(a)(c, p)
                out[k, 2 * j] = x[:, 0:128]
                out[k, 2 * j + 1] = x[:, 128:256]
                tails.append(x[:, 256:320])
            out[k, 4] = jnp.concatenate(tails, axis=1)


def pack(depth, e, h):
    up = len(plane_list(depth, True)) // 2
    dn = len(plane_list(depth, False)) // 2
    return pl.pallas_call(
        lambda *refs: pack_body(depth, *refs),
        out_shape=(
            jax.ShapeDtypeStruct((up, 5, 16, 128), F32),
            jax.ShapeDtypeStruct((dn, 5, 16, 128), F32),
        ),
        in_specs=[HBM] * 2,
        out_specs=[pl.BlockSpec(memory_space=pltpu.VMEM)] * 2,
        scratch_shapes=[
            pltpu.VMEM((2, 3, depth, NY, NZ), F32),
            pltpu.VMEM((2, 3, depth, NY, NZ), F32),
            pltpu.SemaphoreType.DMA((4,)),
        ],
        compiler_params=pltpu.CompilerParams(vmem_limit_bytes=60 << 20),
    )(e, h)


def unpack(depth, buf, upward, put):
    planes = plane_list(depth, upward)
    for k in range(len(planes) // 2):
        tail = buf[k, 4]
        low = lax.broadcasted_iota(jnp.int32, (16, 128), 1) < 64
        tails = (jnp.where(low, tail, 0.0), jnp.where(low, pltpu.roll(tail, 64, 1), 0.0))
        for j in range(2):
            a, c, p = planes[2 * k + j]
            if a == 2:
                put(1, c, GHOST - depth, (buf[k, 2 * j], buf[k, 2 * j + 1], tails[j]))
                continue
            place = p - NX + GHOST if upward else p + NX + GHOST
            put(a, c, place, (buf[k, 2 * j], buf[k, 2 * j + 1], tails[j]))


def widen(x):
    return (x[:, 0:128], x[:, 128:256], jnp.concatenate([x[:, 256:320], jnp.zeros((16, 64), F32)], axis=1))


def store(ref, index, tiles):
    for k in range(3):
        ref[(*index, slice(None), slice(128 * k, 128 * k + 128))] = tiles[k]


def tiles_of(x):
    return [[x[8 * r : 8 * r + 8, 128 * k : 128 * k + 128] for k in range(3)] for r in range(2)]


def joined(v):
    return jnp.concatenate([jnp.concatenate(row, axis=1) for row in v], axis=0)


class Shifts:
    def __init__(self):
        lane = lax.broadcasted_iota(jnp.int32, (8, 128), 1)
        row = lax.broadcasted_iota(jnp.int32, (8, 128), 0)
        self.first_lane, self.last_lane = lane == 0, lane == 127
        self.first_row, self.last_row = row == 0, row == 7

    def ahead_z(self, v):
        out = []
        for r in range(2):
            m = [pltpu.roll(t, 127, 1) for t in v[r]]
            out.append([jnp.where(self.last_lane, m[1], m[0]), jnp.where(self.last_lane, m[2], m[1]), m[2]])
        return out

    def behind_z(self, v):
        out = []
        for r in range(2):
            m = [pltpu.roll(t, 1, 1) for t in v[r]]
            out.append([jnp.where(self.first_lane, 0.0, m[0])] + [jnp.where(self.first_lane, m[k - 1], m[k]) for k in (1, 2)])
        return out

    def ahead_y(self, v):
        m = [[pltpu.roll(t, 7, 0) for t in row] for row in v]
        return [
            [jnp.where(self.last_row, m[1][k], m[0][k]) for k in range(3)],
            [jnp.where(self.last_row, 0.0, m[1][k]) for k in range(3)],
        ]

    def behind_y(self, v):
        m = [[pltpu.roll(t, 1, 0) for t in row] for row in v]
        return [
            [jnp.where(self.first_row, 0.0, m[0][k]) for k in range(3)],
            [jnp.where(self.first_row, m[0][k], m[1][k]) for k in range(3)],
        ]


def each(fn, *vs):
    return [[fn(*(v[r][k] for v in vs)) for k in range(3)] for r in range(2)]


def h_phase(sh, e_at, h_ref, ez_ref, hz_ref, q):
    e = [[tiles_of(e_at(c, q + d)) for c in range(3)] for d in range(2)]
    e.append([None] + [tiles_of(e_at(c, q + 2)) for c in (1, 2)])
    for d in range(2):
        here, then = e[d], e[d + 1]
        z0, z1 = (tiles_of(ez_ref[c, q + d]) for c in range(2))
        y2, y0 = sh.ahead_y(here[2]), sh.ahead_y(here[0])
        h = [tiles_of(h_ref[c, q + d]) for c in range(3)]
        f = lambda h, a, b, c, d: h - ((a - b) - (c - d))
        h = (
            each(f, h[0], y2, here[2], z1, here[1]),
            each(f, h[1], z0, here[0], then[2], here[2]),
            each(f, h[2], then[1], here[1], y0, here[0]),
        )
        for c in range(3):
            h_ref[c, q + d] = joined(h[c])
        for c in range(2):
            hz_ref[c, q + d] = joined(sh.behind_z(h[c]))


def e_phase(sh, e_at, e_put, h_ref, hz_ref, ci_ref, q, use):
    before = [None] + [tiles_of(h_ref[c, q - 1]) for c in (1, 2)]
    f = lambda a, b, c, d: (a - b) - (c - d)
    for d in range(2):
        h = [tiles_of(h_ref[c, q + d]) for c in range(3)]
        z0, z1 = (tiles_of(hz_ref[c, q + d]) for c in range(2))
        y2, y0 = sh.behind_y(h[2]), sh.behind_y(h[0])
        curl = (
            each(f, h[2], y2, h[1], z1),
            each(f, h[0], z0, h[2], before[2]),
            each(f, h[1], before[1], h[0], y0),
        )
        ci = tiles_of(ci_ref[q + d])
        for c in range(3):
            e_put(c, q + d, joined(each(lambda x, k, y: x + k * y, tiles_of(e_at(c, q + d)), ci, curl[c])))
        if use is not None:
            use(q + d, curl)
        before = h


def sweep(sh, tile, reach, e_at, e_put, e_mirror, h_ref, ez_ref, hz_ref, ci_ref, use):
    @pl.when(tile == 0)
    def _():
        for c in (1, 2):
            e_mirror(c)

    def turn(q, fn):
        for d in range(2):
            for c in range(2):
                ez_ref[c, q + 2 + d] = joined(sh.ahead_z(tiles_of(e_at(c, q + 2 + d))))
        h_phase(sh, e_at, h_ref, ez_ref, hz_ref, q)
        e_phase(sh, e_at, e_put, h_ref, hz_ref, ci_ref, q - 2, fn)

    even = reach + reach % 2
    own, end = GHOST, GHOST + NX
    ranges = ((own - even - 2, own + 2, None), (own + 2, end + 2, use), (end + 2, GHOST + NX + reach - 1 + reach % 2 * 1 + 2, None))
    ranges = ranges[:2] + ((end + 2, end + even + 2 if reach % 2 == 0 else end + reach + 1, None),)
    for start, stop, fn in ranges:
        if stop > start:
            @pl.loop(0, (stop - start) // 2)
            def _(i, start=start, fn=fn):
                turn(start + 2 * i, fn)


def stage(refs, *staged):
    copies = [pltpu.make_async_copy(ref, place, staged[-1].at[k]) for k, (ref, place) in enumerate(zip(refs, staged))]
    for copy in copies:
        copy.start()

    def ready(*which):
        for k in which:
            copies[k].wait()

    return (*staged[:-1], ready)


def staging(*arrays):
    return [pltpu.VMEM(x.shape, F32) for x in arrays] + [pltpu.SemaphoreType.DMA((len(arrays),))]


def fill_inverse(perm_ref, ci_ref):
    places = [(s, 0, GHOST + s) for s in range(NX)]
    places += [(s, 1, GHOST + NX + s) for s in range(DEEP - 1)]
    places += [(s, 1, s - NX + GHOST) for s in range(NX - DEEP + 1, NX)]
    for s, which, place in places:
        t = widen(perm_ref[s, which])
        store(ci_ref, (place,), [jnp.where(x > 0, (courant * courant) / jnp.where(x > 0, x, 1.0), 0.0) for x in t])


def adjoint_body(tile_ref, perm_ref, a_ref, b_ref, up_ref, dn_ref, hist_ref, ci_ref, h_ref, e_ref, ez_ref, hz_ref, sem, *staged):
    sh = Shifts()
    tile = tile_ref[0]
    depth = STEPS - 1
    perm_ref, a_ref, b_ref, up_ref, dn_ref, ready = stage((perm_ref, a_ref, b_ref, up_ref, dn_ref), *staged)
    ready(0)
    fill_inverse(perm_ref, ci_ref)
    ready(1, 2)

    def put(a, c, place, t):
        if a == 1:
            store(h_ref, (c, place), [x * (-1.0 / courant) for x in t])
        else:
            ci = ci_ref[place]
            store(e_ref, (0, c, place), [t[k] * ci[:, 128 * k : 128 * k + 128] * (1.0 / (courant * courant)) for k in range(3)])

    for c in range(3):
        @pl.loop(0, NX)
        def _(p):
            put(0, c, p + GHOST, widen(a_ref[0, c, p]))
            put(1, c, p + GHOST, widen(b_ref[0, c, p]))
    ready(3, 4)
    unpack(depth, up_ref, True, put)
    unpack(depth, dn_ref, False, put)

    def out(j):
        return pltpu.make_async_copy(e_ref.at[j, :, pl.ds(GHOST, NX)], hist_ref.at[j], sem.at[j])

    out(0).start()
    for j in range(depth):
        def e_put(c, p, x, j=j):
            e_ref[j + 1, c, p] = x

        def e_mirror(c, j=j):
            e_ref[j, c, GHOST - 1] = e_ref[j, c, GHOST]

        sweep(sh, tile, depth - j, lambda c, p, j=j: e_ref[j, c, p], e_put, e_mirror, h_ref, ez_ref, hz_ref, ci_ref, None)
        out(j + 1).start()
    for j in range(depth + 1):
        out(j).wait()


def forward_body(tile_ref, perm_ref, e0_ref, h0_ref, up_ref, dn_ref, hist_ref, efin_ref, sum_ref, ci_ref, h_ref, e_ref, ahat_ref, ez_ref, hz_ref, sem, *staged):
    sh = Shifts()
    tile = tile_ref[0]
    depth = STEPS

    def fetch(j):
        return pltpu.make_async_copy(hist_ref.at[j], ahat_ref.at[j], sem.at[j])

    perm_ref, e0_ref, h0_ref, up_ref, dn_ref, ready = stage((perm_ref, e0_ref, h0_ref, up_ref, dn_ref), *staged)
    for t in range(STEPS):
        fetch(STEPS - 1 - t).start()
    ready(0)
    fill_inverse(perm_ref, ci_ref)
    ready(1, 2)

    def put(a, c, place, t):
        if a == 1:
            store(h_ref, (c, place), [x * (1.0 / courant) for x in t])
        else:
            store(e_ref, (c, place), t)

    for c in range(3):
        @pl.loop(0, NX)
        def _(p):
            put(0, c, p + GHOST, widen(e0_ref[0, c, p]))
            put(1, c, p + GHOST, widen(h0_ref[0, c, p]))
    ready(3, 4)
    unpack(depth, up_ref, True, put)
    unpack(depth, dn_ref, False, put)
    last = GHOST - depth
    e_ref[0, last] = jnp.zeros((NY, WIDE), F32)
    for c in (1, 2):
        e_ref[c, last] = e_ref[c, last + 1]

    def e_put(c, p, x):
        e_ref[c, p] = x

    def e_mirror(c):
        e_ref[c, GHOST - 1] = e_ref[c, GHOST]

    for t in range(STEPS):
        fetch(STEPS - 1 - t).wait()

        def use(p, curl, t=t):
            q = p - GHOST
            a = [tiles_of(ahat_ref[STEPS - 1 - t, c, q]) for c in range(3)]
            s = each(lambda x0, y0, x1, y1, x2, y2: x0 * y0 + x1 * y1 + x2 * y2, a[0], curl[0], a[1], curl[1], a[2], curl[2])
            s = joined(s)
            if t > 0:
                s = s + sum_ref[q]
            sum_ref[q] = s

        sweep(sh, tile, depth - t, lambda c, p: e_ref[c, p], e_put, e_mirror, h_ref, ez_ref, hz_ref, ci_ref, use)
    for c in range(3):
        @pl.loop(0, NX)
        def _(p):
            efin_ref[0, c, p] = e_ref[c, p + GHOST][:, :NZ]


VM = pl.BlockSpec(memory_space=pltpu.VMEM)
HBM = pl.BlockSpec(memory_space=pltpu.HBM)
SM = pl.BlockSpec(memory_space=pltpu.SMEM)
FIELD = (3, ALL, NY, WIDE)


def adjoint(tile, perm, a, b, up, dn, interpret=False):
    return pl.pallas_call(
        adjoint_body,
        out_shape=jax.ShapeDtypeStruct((STEPS, 3, NX, NY, WIDE), F32),
        in_specs=[SM] + [HBM] * 5,
        out_specs=HBM,
        scratch_shapes=[
            pltpu.VMEM((ALL, NY, WIDE), F32),
            pltpu.VMEM(FIELD, F32),
            pltpu.VMEM((STEPS, *FIELD), F32),
            pltpu.VMEM((2, ALL, NY, WIDE), F32),
            pltpu.VMEM((2, ALL, NY, WIDE), F32),
            pltpu.SemaphoreType.DMA((STEPS,)),
            *staging(perm, a, b, up, dn),
        ],
        compiler_params=pltpu.CompilerParams(vmem_limit_bytes=44 << 20),
        name="adjoint",
        interpret=interpret,
    )(tile, perm, a, b, up, dn)


def forward(tile, perm, e, h, up, dn, hist, interpret=False):
    return pl.pallas_call(
        forward_body,
        out_shape=(
            jax.ShapeDtypeStruct((1, 3, NX, NY, NZ), F32),
            jax.ShapeDtypeStruct((NX, NY, WIDE), F32),
        ),
        in_specs=[SM] + [HBM] * 6,
        out_specs=(VM, VM),
        scratch_shapes=[
            pltpu.VMEM((ALL, NY, WIDE), F32),
            pltpu.VMEM(FIELD, F32),
            pltpu.VMEM(FIELD, F32),
            pltpu.VMEM((STEPS, 3, NX, NY, WIDE), F32),
            pltpu.VMEM((2, ALL, NY, WIDE), F32),
            pltpu.VMEM((2, ALL, NY, WIDE), F32),
            pltpu.SemaphoreType.DMA((STEPS,)),
            *staging(perm, e, h, up, dn),
        ],
        compiler_params=pltpu.CompilerParams(vmem_limit_bytes=44 << 20),
        name="forward",
        interpret=interpret,
    )(tile, perm, e, h, up, dn, hist)


def on_device(permittivity, e_start, h_start, e_cotangent, h_cotangent):
    tiles, sources = lax.axis_size("tile"), lax.axis_size("src")
    tile = lax.axis_index("tile").astype(jnp.int32).reshape(1)
    upward = [(i, i + 1) for i in range(tiles - 1)]
    downward = [(i + 1, i) for i in range(tiles - 1)]
    near = [(t * sources + s, (t - 1) * sources + s) for t in range(1, tiles) for s in range(DEEP - 1)]
    near += [(t * sources + s, (t + 1) * sources + s) for t in range(tiles - 1) for s in range(NX - DEEP + 1, NX)]

    border = lax.ppermute(permittivity, ("tile", "src"), near)
    a_up, a_dn = pack(STEPS - 1, e_cotangent, h_cotangent)
    a_up = lax.ppermute(a_up, "tile", upward)
    a_dn = lax.ppermute(a_dn, "tile", downward)
    both = jnp.concatenate([permittivity, border], axis=0)
    perm = lax.all_to_all(jnp.broadcast_to(both, (sources, *both.shape)), "src", 0, 0, tiled=True)
    e_up, e_dn = pack(STEPS, e_start, h_start)
    e_up = lax.ppermute(e_up, "tile", upward)
    e_dn = lax.ppermute(e_dn, "tile", downward)
    hist = adjoint(tile, perm, e_cotangent, h_cotangent, a_up, a_dn)
    e_final, sums = forward(tile, perm, e_start, h_start, e_up, e_dn, hist)
    parts = lax.all_to_all(sums, "src", 0, 0, tiled=True)
    total = jnp.sum(parts, axis=0, keepdims=True)[:, :, :NZ]
    gradient = -(courant * courant) * total / permittivity
    return e_final, gradient


def solution(mesh):
    field = P("src", None, "tile", None, None)
    in_specs = (P(("tile", "src"), None, None), field, field, field, field)
    out_specs = (field, P(("tile", "src"), None, None))

    return jax.shard_map(on_device, mesh=mesh, in_specs=in_specs, out_specs=out_specs, check_vma=False)
```

profile of v0, /device:TPU:96, one launch (start us, length us, event | category | flops | bytes accessed | tf_op | source)
XLA Modules:
  0.0 98.6 jit_solution(15417365668905006190)
XLA Ops:
  0.6 2.3 %collective-permute-start = (f32[1,16,320]{2,1,0:T(8,128)}, f32[1,16,320]{2,1,0:T(8,128)S(1)}, u32[]{:S(2)}, u32[]{:S(2)}) collective-permute-start(f32[1,16,320]{2,1,0:T(8,128)} %param.5), channel_id=1, source_target_pairs={{16,0},{17,1},{18,2},{19,3},{20,4},{32,16},{33,17},{34,18},{35,19}... | collective-permute-start | bytes 61448 | tf_op jit(solution)/shard_map/ppermute | solution.py:411
  2.9 2.4 %shard_map.69 = (f32[15,5,16,128]{3,2,1,0:T(8,128)}, f32[13,5,16,128]{3,2,1,0:T(8,128)}) custom-call(f32[1,3,16,16,320]{4,3,2,1,0:T(8,128)} %a_ref.1, f32[1,3,16,16,320]{4,3,2,1,0:T(8,128)} %b_ref.1), custom_call_target="tpu_custom_call" | custom-call | tf_op jit(solution)/shard_map/pallas_call | solution.py:72
  5.3 0.0 copy-start.4
  5.3 7.1 %collective-permute-start.3 = (f32[15,5,16,128]{3,2,1,0:T(8,128)}, f32[15,5,16,128]{3,2,1,0:T(8,128)}, u32[]{:S(2)}, u32[]{:S(2)}) collective-permute-start(f32[15,5,16,128]{3,2,1,0:T(8,128)} %get-tuple-element.10), channel_id=1, source_target_pairs={{0,16},{16,32},{32,48},{48,64},{64,80},{80,96},{96,112},{1,17},{17... | collective-permute-start | bytes 1843208 | tf_op jit(solution)/shard_map/ppermute | solution.py:413
  12.5 2.6 %shard_map.68 = (f32[16,5,16,128]{3,2,1,0:T(8,128)}, f32[16,5,16,128]{3,2,1,0:T(8,128)}) custom-call(f32[1,3,16,16,320]{4,3,2,1,0:T(8,128)} %e0_ref.1, f32[1,3,16,16,320]{4,3,2,1,0:T(8,128)} %h0_ref.1), custom_call_target="tpu_custom_call" | custom-call | tf_op jit(solution)/shard_map/pallas_call | solution.py:72
  15.1 1.9 %collective-permute-start.1 = (f32[16,5,16,128]{3,2,1,0:T(8,128)}, f32[16,5,16,128]{3,2,1,0:T(8,128)}, u32[]{:S(2)}, u32[]{:S(2)}) collective-permute-start(f32[16,5,16,128]{3,2,1,0:T(8,128)} %get-tuple-element.8), channel_id=1, source_target_pairs={{0,16},{16,32},{32,48},{48,64},{64,80},{80,96},{96,112},{1,17},{17... | collective-permute-start | bytes 1966088 | tf_op jit(solution)/shard_map/ppermute | solution.py:418
  17.0 3.9 %collective-permute-start.2 = (f32[16,5,16,128]{3,2,1,0:T(8,128)}, f32[16,5,16,128]{3,2,1,0:T(8,128)}, u32[]{:S(2)}, u32[]{:S(2)}) collective-permute-start(f32[16,5,16,128]{3,2,1,0:T(8,128)} %get-tuple-element.9), channel_id=1, source_target_pairs={{16,0},{32,16},{48,32},{64,48},{80,64},{96,80},{112,96},{17,1},{33... | collective-permute-start | bytes 1966088 | tf_op jit(solution)/shard_map/ppermute | solution.py:419
  20.9 0.0 collective-permute-done
  20.9 0.0 copy-start.2
  21.0 0.0 copy-start.3
  21.0 1.0 broadcast_in_dim.6
  21.9 3.7 %all-to-all-start = ((f32[16,2,16,320]{3,2,1,0:T(8,128)}), f32[16,2,16,320]{3,2,1,0:T(8,128)S(1)}, u32[]{:S(2)}, u32[]{:S(2)}) async-start(f32[16,2,16,320]{3,2,1,0:T(8,128)} %broadcast_in_dim.6), calls=%async_computation | async-start | bytes 1572864 | tf_op jit(solution)/shard_map/all_to_all | solution.py:416
  25.7 1.9 %collective-permute-start.4 = (f32[13,5,16,128]{3,2,1,0:T(8,128)}, f32[13,5,16,128]{3,2,1,0:T(8,128)}, u32[]{:S(2)}, u32[]{:S(2)}) collective-permute-start(f32[13,5,16,128]{3,2,1,0:T(8,128)} %get-tuple-element.11), channel_id=1, source_target_pairs={{16,0},{32,16},{48,32},{64,48},{80,64},{96,80},{112,96},{17,1},{33... | collective-permute-start | bytes 1597448 | tf_op jit(solution)/shard_map/ppermute | solution.py:414
  27.6 30.9 %collective-permute-done.4.dn_ref = f32[13,5,16,128]{3,2,1,0:T(8,128)} collective-permute-done((f32[13,5,16,128]{3,2,1,0:T(8,128)}, f32[13,5,16,128]{3,2,1,0:T(8,128)}, u32[]{:S(2)}, u32[]{:S(2)}) %collective-permute-start.4) | collective-permute-done | bytes 532512 | tf_op jit(solution)/shard_map/ppermute | solution.py:414
  58.6 0.0 collective-permute-done.3.up_ref
  58.6 0.0 all-to-all-done.perm_ref
  58.6 0.0 copy-start
  58.6 0.0 copy-start.1
  58.6 11.0 %adjoint.1.hist_ref = f32[6,3,16,16,384]{4,3,2,1,0:T(8,128)} custom-call(s32[1]{0:T(128)} %bitcast.tile_ref, f32[16,2,16,320]{3,2,1,0:T(8,128)S(1)} %all-to-all-done.perm_ref, f32[1,3,16,16,320]{4,3,2,1,0:T(8,128)S(1)} %copy-done.2, f32[1,3,16,16,320]{4,3,2,1,0:T(8,128)S(1)} %copy-done.3, f32[15,5,16,128]{3,2,1,0:T(8,128)} %collective-permute-done.3.up_ref, ...), custom_call_target="tpu_custom_call" | custom-call | tf_op jit(solution)/shard_map/adjoint/pallas_call | solution.py:358
  69.6 0.0 collective-permute-done.1.up_ref
  69.6 0.0 collective-permute-done.2.dn_ref
  69.7 15.0 %forward.1 = (f32[1,3,16,16,320]{4,3,2,1,0:T(8,128)}, f32[16,16,384]{2,1,0:T(8,128)S(1)}) custom-call(s32[1]{0:T(128)} %bitcast.tile_ref, f32[16,2,16,320]{3,2,1,0:T(8,128)S(1)} %all-to-all-done.perm_ref, f32[1,3,16,16,320]{4,3,2,1,0:T(8,128)S(1)} %copy-done, f32[1,3,16,16,320]{4,3,2,1,0:T(8,128)S(1)} %copy-done.1, ...), custom_call_target="tpu_custom_call" | custom-call | tf_op jit(solution)/shard_map/forward/pallas_call | solution.py:379
  84.7 13.2 %all_to_all.10 = f32[16,16,384]{2,1,0:T(8,128)S(1)} all-to-all(f32[16,16,384]{2,1,0:T(8,128)S(1)} %get-tuple-element.13), channel_id=1, replica_groups=mesh['tile'=8,'src'=16] {'src'}, dimensions={0} | all-to-all | bytes 786432 | tf_op jit(solution)/shard_map/all_to_all | solution.py:422
  98.0 0.6 fusion
  (7 shorter events, 0.0 us)
Async XLA Ops:
  0.6 20.3 %collective-permute-start = (f32[1,16,320]{2,1,0:T(8,128)}, f32[1,16,320]{2,1,0:T(8,128)S(1)}, u32[]{:S(2)}, u32[]{:S(2)}) collective-permute-start(f32[1,16,320]{2,1,0:T(8,128)} %param.5), channel_id=1, source_target_pairs={{16,0},{17,1},{18,2},{19,3},{20,4},{32,16},{33,17},{34,18},{35,19}... | collective-permute-start | bytes 61448 | tf_op jit(solution)/shard_map/ppermute | solution.py:411
  5.3 15.6 %copy-start.4 = (f32[1,16,320]{2,1,0:T(8,128)S(1)}, f32[1,16,320]{2,1,0:T(8,128)}, u32[]{:S(2)}) copy-start(f32[1,16,320]{2,1,0:T(8,128)} %param.5) | copy-start | bytes 61444
  5.3 53.2 %collective-permute-start.3 = (f32[15,5,16,128]{3,2,1,0:T(8,128)}, f32[15,5,16,128]{3,2,1,0:T(8,128)}, u32[]{:S(2)}, u32[]{:S(2)}) collective-permute-start(f32[15,5,16,128]{3,2,1,0:T(8,128)} %get-tuple-element.10), channel_id=1, source_target_pairs={{0,16},{16,32},{32,48},{48,64},{64,80},{80,96},{96,112},{1,17},{17... | collective-permute-start | bytes 1843208 | tf_op jit(solution)/shard_map/ppermute | solution.py:413
  15.1 54.6 %collective-permute-start.1 = (f32[16,5,16,128]{3,2,1,0:T(8,128)}, f32[16,5,16,128]{3,2,1,0:T(8,128)}, u32[]{:S(2)}, u32[]{:S(2)}) collective-permute-start(f32[16,5,16,128]{3,2,1,0:T(8,128)} %get-tuple-element.8), channel_id=1, source_target_pairs={{0,16},{16,32},{32,48},{48,64},{64,80},{80,96},{96,112},{1,17},{17... | collective-permute-start | bytes 1966088 | tf_op jit(solution)/shard_map/ppermute | solution.py:418
  17.0 52.7 %collective-permute-start.2 = (f32[16,5,16,128]{3,2,1,0:T(8,128)}, f32[16,5,16,128]{3,2,1,0:T(8,128)}, u32[]{:S(2)}, u32[]{:S(2)}) collective-permute-start(f32[16,5,16,128]{3,2,1,0:T(8,128)} %get-tuple-element.9), channel_id=1, source_target_pairs={{16,0},{32,16},{48,32},{64,48},{80,64},{96,80},{112,96},{17,1},{33... | collective-permute-start | bytes 1966088 | tf_op jit(solution)/shard_map/ppermute | solution.py:419
  20.9 37.6 %copy-start.2 = (f32[1,3,16,16,320]{4,3,2,1,0:T(8,128)S(1)}, f32[1,3,16,16,320]{4,3,2,1,0:T(8,128)}, u32[]{:S(2)}) copy-start(f32[1,3,16,16,320]{4,3,2,1,0:T(8,128)} %a_ref.1) | copy-start | bytes 2949124
  21.0 37.6 %copy-start.3 = (f32[1,3,16,16,320]{4,3,2,1,0:T(8,128)S(1)}, f32[1,3,16,16,320]{4,3,2,1,0:T(8,128)}, u32[]{:S(2)}) copy-start(f32[1,3,16,16,320]{4,3,2,1,0:T(8,128)} %b_ref.1) | copy-start | bytes 2949124
  21.9 36.6 %all-to-all-start = ((f32[16,2,16,320]{3,2,1,0:T(8,128)}), f32[16,2,16,320]{3,2,1,0:T(8,128)S(1)}, u32[]{:S(2)}, u32[]{:S(2)}) async-start(f32[16,2,16,320]{3,2,1,0:T(8,128)} %broadcast_in_dim.6), calls=%async_computation | async-start | bytes 1572864 | tf_op jit(solution)/shard_map/all_to_all | solution.py:416
  25.7 32.9 %collective-permute-start.4 = (f32[13,5,16,128]{3,2,1,0:T(8,128)}, f32[13,5,16,128]{3,2,1,0:T(8,128)}, u32[]{:S(2)}, u32[]{:S(2)}) collective-permute-start(f32[13,5,16,128]{3,2,1,0:T(8,128)} %get-tuple-element.11), channel_id=1, source_target_pairs={{16,0},{32,16},{48,32},{64,48},{80,64},{96,80},{112,96},{17,1},{33... | collective-permute-start | bytes 1597448 | tf_op jit(solution)/shard_map/ppermute | solution.py:414
  58.6 11.1 %copy-start = (f32[1,3,16,16,320]{4,3,2,1,0:T(8,128)S(1)}, f32[1,3,16,16,320]{4,3,2,1,0:T(8,128)}, u32[]{:S(2)}) copy-start(f32[1,3,16,16,320]{4,3,2,1,0:T(8,128)} %e0_ref.1) | copy-start | bytes 2949124
  58.6 11.1 %copy-start.1 = (f32[1,3,16,16,320]{4,3,2,1,0:T(8,128)S(1)}, f32[1,3,16,16,320]{4,3,2,1,0:T(8,128)}, u32[]{:S(2)}) copy-start(f32[1,3,16,16,320]{4,3,2,1,0:T(8,128)} %h0_ref.1) | copy-start | bytes 2949124
where the time goes:
time: 99.1 us; the launch traced here: 98.6 us
  Pallas kernels  31 us (31%)
  waiting for transfers between devices  30.9 us (31%)
  starting transfers between devices  21 us (21%)
  blocking collectives  13.2 us (13%)
    ppermute x1, waiting for transfers between devices, on_device(): a_dn = lax.ppermute(a_dn, 'tile', downward)  30.9 us
    pallas_call x1, Pallas kernels, forward(): pl.pallas_call(forward_body, out_shape=(jax.ShapeDtypeStruct((1, 3, NX, N...  15 us
    all_to_all x1, blocking collectives, on_device(): parts = lax.all_to_all(sums, 'src', 0, 0, tiled=True)  13.2 us
    pallas_call x1, Pallas kernels, adjoint(): pl.pallas_call(adjoint_body, out_shape=jax.ShapeDtypeStruct((STEPS, 3, NX...  11 us
    ppermute x1, starting transfers between devices, on_device(): a_up = lax.ppermute(a_up, 'tile', upward)  7.15 us
    pallas_call x2, Pallas kernels, pack(): pl.pallas_call(lambda *refs: pack_body(depth, *refs), out_shape=(jax.Shap...  4.92 us
    ppermute x1, starting transfers between devices, on_device(): e_dn = lax.ppermute(e_dn, 'tile', downward)  3.92 us
    all_to_all x1, starting transfers between devices, on_device(): lax.all_to_all(jnp.broadcast_to(both, (sources, *both.shape)), 'src', 0,...  3.75 us
  transfers between devices with their start and end apart: 6, of which 1 were waited for; matrix products, arithmetic and copies ran while one was open for 1% of the time, Pallas kernels for 16%

commit v1 on v0

--- a/solution.py
+++ b/solution.py
@@ -251,10 +251,8 @@
     sh = Shifts()
     tile = tile_ref[0]
     depth = STEPS - 1
-    perm_ref, a_ref, b_ref, up_ref, dn_ref, ready = stage((perm_ref, a_ref, b_ref, up_ref, dn_ref), *staged)
-    ready(0)
+    up_ref, dn_ref, ready = stage((up_ref, dn_ref), *staged)
     fill_inverse(perm_ref, ci_ref)
-    ready(1, 2)
 
     def put(a, c, place, t):
         if a == 1:
@@ -268,7 +266,7 @@
         def _(p):
             put(0, c, p + GHOST, widen(a_ref[0, c, p]))
             put(1, c, p + GHOST, widen(b_ref[0, c, p]))
-    ready(3, 4)
+    ready(0, 1)
     unpack(depth, up_ref, True, put)
     unpack(depth, dn_ref, False, put)
 
@@ -297,12 +295,10 @@
     def fetch(j):
         return pltpu.make_async_copy(hist_ref.at[j], ahat_ref.at[j], sem.at[j])
 
-    perm_ref, e0_ref, h0_ref, up_ref, dn_ref, ready = stage((perm_ref, e0_ref, h0_ref, up_ref, dn_ref), *staged)
+    up_ref, dn_ref, ready = stage((up_ref, dn_ref), *staged)
     for t in range(STEPS):
         fetch(STEPS - 1 - t).start()
-    ready(0)
     fill_inverse(perm_ref, ci_ref)
-    ready(1, 2)
 
     def put(a, c, place, t):
         if a == 1:
@@ -315,7 +311,7 @@
         def _(p):
             put(0, c, p + GHOST, widen(e0_ref[0, c, p]))
             put(1, c, p + GHOST, widen(h0_ref[0, c, p]))
-    ready(3, 4)
+    ready(0, 1)
     unpack(depth, up_ref, True, put)
     unpack(depth, dn_ref, False, put)
     last = GHOST - depth
@@ -358,7 +354,7 @@
     return pl.pallas_call(
         adjoint_body,
         out_shape=jax.ShapeDtypeStruct((STEPS, 3, NX, NY, WIDE), F32),
-        in_specs=[SM] + [HBM] * 5,
+        in_specs=[SM, VM, VM, VM, HBM, HBM],
         out_specs=HBM,
         scratch_shapes=[
             pltpu.VMEM((ALL, NY, WIDE), F32),
@@ -367,7 +363,7 @@
             pltpu.VMEM((2, ALL, NY, WIDE), F32),
             pltpu.VMEM((2, ALL, NY, WIDE), F32),
             pltpu.SemaphoreType.DMA((STEPS,)),
-            *staging(perm, a, b, up, dn),
+            *staging(up, dn),
         ],
         compiler_params=pltpu.CompilerParams(vmem_limit_bytes=44 << 20),
         name="adjoint",
@@ -382,7 +378,7 @@
             jax.ShapeDtypeStruct((1, 3, NX, NY, NZ), F32),
             jax.ShapeDtypeStruct((NX, NY, WIDE), F32),
         ),
-        in_specs=[SM] + [HBM] * 6,
+        in_specs=[SM, VM, VM, VM, HBM, HBM, HBM],
         out_specs=(VM, VM),
         scratch_shapes=[
             pltpu.VMEM((ALL, NY, WIDE), F32),
@@ -392,7 +388,7 @@
             pltpu.VMEM((2, ALL, NY, WIDE), F32),
             pltpu.VMEM((2, ALL, NY, WIDE), F32),
             pltpu.SemaphoreType.DMA((STEPS,)),
-            *staging(perm, e, h, up, dn),
+            *staging(up, dn),
         ],
         compiler_params=pltpu.CompilerParams(vmem_limit_bytes=44 << 20),
         name="forward",

time: 99.1 us -> 97.9 us (0.988)
  Pallas kernels: 31 us -> 29.9 us
where the time goes in v1:
time: 97.9 us; the launch traced here: 97.5 us
  waiting for transfers between devices  30.9 us (32%)
  Pallas kernels  29.9 us (31%)
  starting transfers between devices  21 us (21%)
  blocking collectives  13.2 us (13%)
  local copies, waits for them, and re-layouts  0.99 us (1%)
    ppermute x1, waiting for transfers between devices, on_device(): a_dn = lax.ppermute(a_dn, 'tile', downward)  30.9 us
    pallas_call x1, Pallas kernels, forward(): pl.pallas_call(forward_body, out_shape=(jax.ShapeDtypeStruct((1, 3, NX, N...  14.5 us
    all_to_all x1, blocking collectives, on_device(): parts = lax.all_to_all(sums, 'src', 0, 0, tiled=True)  13.2 us
    pallas_call x1, Pallas kernels, adjoint(): pl.pallas_call(adjoint_body, out_shape=jax.ShapeDtypeStruct((STEPS, 3, NX...  10.5 us
    ppermute x1, starting transfers between devices, on_device(): a_up = lax.ppermute(a_up, 'tile', upward)  7.15 us
    pallas_call x2, Pallas kernels, pack(): pl.pallas_call(lambda *refs: pack_body(depth, *refs), out_shape=(jax.Shap...  4.92 us
    ppermute x1, starting transfers between devices, on_device(): e_dn = lax.ppermute(e_dn, 'tile', downward)  3.92 us
    all_to_all x1, starting transfers between devices, on_device(): lax.all_to_all(jnp.broadcast_to(both, (sources, *both.shape)), 'src', 0,...  3.75 us
  transfers between devices with their start and end apart: 6, of which 1 were waited for; matrix products, arithmetic and copies ran while one was open for 1% of the time, Pallas kernels for 16%

profile of v1, /device:TPU:96, one launch (start us, length us, event | category | flops | bytes accessed | tf_op | source)
XLA Modules:
  0.0 97.5 jit_solution(8813784175758616927)
XLA Ops:
  0.6 2.3 %collective-permute-start = (f32[1,16,320]{2,1,0:T(8,128)}, f32[1,16,320]{2,1,0:T(8,128)S(1)}, u32[]{:S(2)}, u32[]{:S(2)}) collective-permute-start(f32[1,16,320]{2,1,0:T(8,128)} %param.5), channel_id=1, source_target_pairs={{16,0},{17,1},{18,2},{19,3},{20,4},{32,16},{33,17},{34,18},{35,19}... | collective-permute-start | bytes 61448 | tf_op jit(solution)/shard_map/ppermute | solution.py:407
  2.9 2.4 %shard_map.69 = (f32[15,5,16,128]{3,2,1,0:T(8,128)}, f32[13,5,16,128]{3,2,1,0:T(8,128)}) custom-call(f32[1,3,16,16,320]{4,3,2,1,0:T(8,128)} %a_ref.1, f32[1,3,16,16,320]{4,3,2,1,0:T(8,128)} %b_ref.1), custom_call_target="tpu_custom_call" | custom-call | tf_op jit(solution)/shard_map/pallas_call | solution.py:72
  5.3 0.0 copy-start.4
  5.3 7.1 %collective-permute-start.3 = (f32[15,5,16,128]{3,2,1,0:T(8,128)}, f32[15,5,16,128]{3,2,1,0:T(8,128)}, u32[]{:S(2)}, u32[]{:S(2)}) collective-permute-start(f32[15,5,16,128]{3,2,1,0:T(8,128)} %get-tuple-element.10), channel_id=1, source_target_pairs={{0,16},{16,32},{32,48},{48,64},{64,80},{80,96},{96,112},{1,17},{17... | collective-permute-start | bytes 1843208 | tf_op jit(solution)/shard_map/ppermute | solution.py:409
  12.5 2.6 %shard_map.68 = (f32[16,5,16,128]{3,2,1,0:T(8,128)}, f32[16,5,16,128]{3,2,1,0:T(8,128)}) custom-call(f32[1,3,16,16,320]{4,3,2,1,0:T(8,128)} %e0_ref.1, f32[1,3,16,16,320]{4,3,2,1,0:T(8,128)} %h0_ref.1), custom_call_target="tpu_custom_call" | custom-call | tf_op jit(solution)/shard_map/pallas_call | solution.py:72
  15.1 1.9 %collective-permute-start.1 = (f32[16,5,16,128]{3,2,1,0:T(8,128)}, f32[16,5,16,128]{3,2,1,0:T(8,128)}, u32[]{:S(2)}, u32[]{:S(2)}) collective-permute-start(f32[16,5,16,128]{3,2,1,0:T(8,128)} %get-tuple-element.8), channel_id=1, source_target_pairs={{0,16},{16,32},{32,48},{48,64},{64,80},{80,96},{96,112},{1,17},{17... | collective-permute-start | bytes 1966088 | tf_op jit(solution)/shard_map/ppermute | solution.py:414
  17.0 3.9 %collective-permute-start.2 = (f32[16,5,16,128]{3,2,1,0:T(8,128)}, f32[16,5,16,128]{3,2,1,0:T(8,128)}, u32[]{:S(2)}, u32[]{:S(2)}) collective-permute-start(f32[16,5,16,128]{3,2,1,0:T(8,128)} %get-tuple-element.9), channel_id=1, source_target_pairs={{16,0},{32,16},{48,32},{64,48},{80,64},{96,80},{112,96},{17,1},{33... | collective-permute-start | bytes 1966088 | tf_op jit(solution)/shard_map/ppermute | solution.py:415
  20.9 0.0 collective-permute-done
  20.9 0.0 copy-start.2
  21.0 0.0 copy-start.3
  21.0 1.0 broadcast_in_dim.6
  21.9 3.7 %all-to-all-start = ((f32[16,2,16,320]{3,2,1,0:T(8,128)}), f32[16,2,16,320]{3,2,1,0:T(8,128)S(1)}, u32[]{:S(2)}, u32[]{:S(2)}) async-start(f32[16,2,16,320]{3,2,1,0:T(8,128)} %broadcast_in_dim.6), calls=%async_computation | async-start | bytes 1572864 | tf_op jit(solution)/shard_map/all_to_all | solution.py:412
  25.7 1.9 %collective-permute-start.4 = (f32[13,5,16,128]{3,2,1,0:T(8,128)}, f32[13,5,16,128]{3,2,1,0:T(8,128)}, u32[]{:S(2)}, u32[]{:S(2)}) collective-permute-start(f32[13,5,16,128]{3,2,1,0:T(8,128)} %get-tuple-element.11), channel_id=1, source_target_pairs={{16,0},{32,16},{48,32},{64,48},{80,64},{96,80},{112,96},{17,1},{33... | collective-permute-start | bytes 1597448 | tf_op jit(solution)/shard_map/ppermute | solution.py:410
  27.6 30.9 %collective-permute-done.4.dn_ref = f32[13,5,16,128]{3,2,1,0:T(8,128)} collective-permute-done((f32[13,5,16,128]{3,2,1,0:T(8,128)}, f32[13,5,16,128]{3,2,1,0:T(8,128)}, u32[]{:S(2)}, u32[]{:S(2)}) %collective-permute-start.4) | collective-permute-done | bytes 532512 | tf_op jit(solution)/shard_map/ppermute | solution.py:410
  58.6 0.0 collective-permute-done.3.up_ref
  58.6 0.0 all-to-all-done.perm_ref
  58.6 0.0 copy-start
  58.6 0.0 copy-start.1
  58.6 10.5 %adjoint.1.hist_ref = f32[6,3,16,16,384]{4,3,2,1,0:T(8,128)} custom-call(s32[1]{0:T(128)} %bitcast.tile_ref, f32[16,2,16,320]{3,2,1,0:T(8,128)S(1)} %all-to-all-done.perm_ref, f32[1,3,16,16,320]{4,3,2,1,0:T(8,128)S(1)} %copy-done.2, f32[1,3,16,16,320]{4,3,2,1,0:T(8,128)S(1)} %copy-done.3, f32[15,5,16,128]{3,2,1,0:T(8,128)} %collective-permute-done.3.up_ref, ...), custom_call_target="tpu_custom_call" | custom-call | tf_op jit(solution)/shard_map/adjoint/pallas_call | solution.py:354
  69.1 0.0 collective-permute-done.1.up_ref
  69.1 0.0 collective-permute-done.2.dn_ref
  69.1 14.5 %forward.1 = (f32[1,3,16,16,320]{4,3,2,1,0:T(8,128)}, f32[16,16,384]{2,1,0:T(8,128)S(1)}) custom-call(s32[1]{0:T(128)} %bitcast.tile_ref, f32[16,2,16,320]{3,2,1,0:T(8,128)S(1)} %all-to-all-done.perm_ref, f32[1,3,16,16,320]{4,3,2,1,0:T(8,128)S(1)} %copy-done, f32[1,3,16,16,320]{4,3,2,1,0:T(8,128)S(1)} %copy-done.1, ...), custom_call_target="tpu_custom_call" | custom-call | tf_op jit(solution)/shard_map/forward/pallas_call | solution.py:375
  83.6 13.2 %all_to_all.10 = f32[16,16,384]{2,1,0:T(8,128)S(1)} all-to-all(f32[16,16,384]{2,1,0:T(8,128)S(1)} %get-tuple-element.13), channel_id=1, replica_groups=mesh['tile'=8,'src'=16] {'src'}, dimensions={0} | all-to-all | bytes 786432 | tf_op jit(solution)/shard_map/all_to_all | solution.py:418
  96.8 0.6 fusion
  (7 shorter events, 0.0 us)
Async XLA Ops:
  0.6 20.3 %collective-permute-start = (f32[1,16,320]{2,1,0:T(8,128)}, f32[1,16,320]{2,1,0:T(8,128)S(1)}, u32[]{:S(2)}, u32[]{:S(2)}) collective-permute-start(f32[1,16,320]{2,1,0:T(8,128)} %param.5), channel_id=1, source_target_pairs={{16,0},{17,1},{18,2},{19,3},{20,4},{32,16},{33,17},{34,18},{35,19}... | collective-permute-start | bytes 61448 | tf_op jit(solution)/shard_map/ppermute | solution.py:407
  5.3 15.6 %copy-start.4 = (f32[1,16,320]{2,1,0:T(8,128)S(1)}, f32[1,16,320]{2,1,0:T(8,128)}, u32[]{:S(2)}) copy-start(f32[1,16,320]{2,1,0:T(8,128)} %param.5) | copy-start | bytes 61444
  5.3 53.2 %collective-permute-start.3 = (f32[15,5,16,128]{3,2,1,0:T(8,128)}, f32[15,5,16,128]{3,2,1,0:T(8,128)}, u32[]{:S(2)}, u32[]{:S(2)}) collective-permute-start(f32[15,5,16,128]{3,2,1,0:T(8,128)} %get-tuple-element.10), channel_id=1, source_target_pairs={{0,16},{16,32},{32,48},{48,64},{64,80},{80,96},{96,112},{1,17},{17... | collective-permute-start | bytes 1843208 | tf_op jit(solution)/shard_map/ppermute | solution.py:409
  15.1 54.0 %collective-permute-start.1 = (f32[16,5,16,128]{3,2,1,0:T(8,128)}, f32[16,5,16,128]{3,2,1,0:T(8,128)}, u32[]{:S(2)}, u32[]{:S(2)}) collective-permute-start(f32[16,5,16,128]{3,2,1,0:T(8,128)} %get-tuple-element.8), channel_id=1, source_target_pairs={{0,16},{16,32},{32,48},{48,64},{64,80},{80,96},{96,112},{1,17},{17... | collective-permute-start | bytes 1966088 | tf_op jit(solution)/shard_map/ppermute | solution.py:414
  17.0 52.1 %collective-permute-start.2 = (f32[16,5,16,128]{3,2,1,0:T(8,128)}, f32[16,5,16,128]{3,2,1,0:T(8,128)}, u32[]{:S(2)}, u32[]{:S(2)}) collective-permute-start(f32[16,5,16,128]{3,2,1,0:T(8,128)} %get-tuple-element.9), channel_id=1, source_target_pairs={{16,0},{32,16},{48,32},{64,48},{80,64},{96,80},{112,96},{17,1},{33... | collective-permute-start | bytes 1966088 | tf_op jit(solution)/shard_map/ppermute | solution.py:415
  20.9 37.6 %copy-start.2 = (f32[1,3,16,16,320]{4,3,2,1,0:T(8,128)S(1)}, f32[1,3,16,16,320]{4,3,2,1,0:T(8,128)}, u32[]{:S(2)}) copy-start(f32[1,3,16,16,320]{4,3,2,1,0:T(8,128)} %a_ref.1) | copy-start | bytes 2949124
  21.0 37.6 %copy-start.3 = (f32[1,3,16,16,320]{4,3,2,1,0:T(8,128)S(1)}, f32[1,3,16,16,320]{4,3,2,1,0:T(8,128)}, u32[]{:S(2)}) copy-start(f32[1,3,16,16,320]{4,3,2,1,0:T(8,128)} %b_ref.1) | copy-start | bytes 2949124
  21.9 36.6 %all-to-all-start = ((f32[16,2,16,320]{3,2,1,0:T(8,128)}), f32[16,2,16,320]{3,2,1,0:T(8,128)S(1)}, u32[]{:S(2)}, u32[]{:S(2)}) async-start(f32[16,2,16,320]{3,2,1,0:T(8,128)} %broadcast_in_dim.6), calls=%async_computation | async-start | bytes 1572864 | tf_op jit(solution)/shard_map/all_to_all | solution.py:412
  25.7 32.9 %collective-permute-start.4 = (f32[13,5,16,128]{3,2,1,0:T(8,128)}, f32[13,5,16,128]{3,2,1,0:T(8,128)}, u32[]{:S(2)}, u32[]{:S(2)}) collective-permute-start(f32[13,5,16,128]{3,2,1,0:T(8,128)} %get-tuple-element.11), channel_id=1, source_target_pairs={{16,0},{32,16},{48,32},{64,48},{80,64},{96,80},{112,96},{17,1},{33... | collective-permute-start | bytes 1597448 | tf_op jit(solution)/shard_map/ppermute | solution.py:410
  58.6 10.5 %copy-start = (f32[1,3,16,16,320]{4,3,2,1,0:T(8,128)S(1)}, f32[1,3,16,16,320]{4,3,2,1,0:T(8,128)}, u32[]{:S(2)}) copy-start(f32[1,3,16,16,320]{4,3,2,1,0:T(8,128)} %e0_ref.1) | copy-start | bytes 2949124
  58.6 10.5 %copy-start.1 = (f32[1,3,16,16,320]{4,3,2,1,0:T(8,128)S(1)}, f32[1,3,16,16,320]{4,3,2,1,0:T(8,128)}, u32[]{:S(2)}) copy-start(f32[1,3,16,16,320]{4,3,2,1,0:T(8,128)} %h0_ref.1) | copy-start | bytes 2949124

commit v2 on v1

--- a/solution.py
+++ b/solution.py
@@ -158,10 +158,16 @@
     return [[fn(*(v[r][k] for v in vs)) for k in range(3)] for r in range(2)]
 
 
-def h_phase(sh, e_at, h_ref, ez_ref, hz_ref, q):
-    e = [[tiles_of(e_at(c, q + d)) for c in range(3)] for d in range(2)]
-    e.append([None] + [tiles_of(e_at(c, q + 2)) for c in (1, 2)])
-    for d in range(2):
+def z_phase(sh, e_at, ez_ref, planes):
+    for p in planes:
+        for c in range(2):
+            ez_ref[c, p] = joined(sh.ahead_z(tiles_of(e_at(c, p))))
+
+
+def h_phase(sh, e_at, h_ref, ez_ref, hz_ref, q, count=2):
+    e = [[tiles_of(e_at(c, q + d)) for c in range(3)] for d in range(count)]
+    e.append([None] + [tiles_of(e_at(c, q + count)) for c in (1, 2)])
+    for d in range(count):
         here, then = e[d], e[d + 1]
         z0, z1 = (tiles_of(ez_ref[c, q + d]) for c in range(2))
         y2, y0 = sh.ahead_y(here[2]), sh.ahead_y(here[0])
@@ -178,7 +184,7 @@
             hz_ref[c, q + d] = joined(sh.behind_z(h[c]))
 
 
-def e_phase(sh, e_at, e_put, h_ref, hz_ref, ci_ref, q, use):
+def e_phase(sh, e_at, e_put, h_ref, hz_ref, ci_at, q, use):
     before = [None] + [tiles_of(h_ref[c, q - 1]) for c in (1, 2)]
     f = lambda a, b, c, d: (a - b) - (c - d)
     for d in range(2):
@@ -190,7 +196,7 @@
             each(f, h[0], z0, h[2], before[2]),
             each(f, h[1], before[1], h[0], y0),
         )
-        ci = tiles_of(ci_ref[q + d])
+        ci = tiles_of(ci_at(q + d))
         for c in range(3):
             e_put(c, q + d, joined(each(lambda x, k, y: x + k * y, tiles_of(e_at(c, q + d)), ci, curl[c])))
         if use is not None:
@@ -198,23 +204,21 @@
         before = h
 
 
-def sweep(sh, tile, reach, e_at, e_put, e_mirror, h_ref, ez_ref, hz_ref, ci_ref, use):
+def sweep(sh, tile, reach, e_at, e_put, e_mirror, h_ref, ez_ref, hz_ref, ci_at, use):
     @pl.when(tile == 0)
     def _():
         for c in (1, 2):
             e_mirror(c)
 
     def turn(q, fn):
-        for d in range(2):
-            for c in range(2):
-                ez_ref[c, q + 2 + d] = joined(sh.ahead_z(tiles_of(e_at(c, q + 2 + d))))
+        z_phase(sh, e_at, ez_ref, (q + 2, q + 3))
         h_phase(sh, e_at, h_ref, ez_ref, hz_ref, q)
-        e_phase(sh, e_at, e_put, h_ref, hz_ref, ci_ref, q - 2, fn)
+        e_phase(sh, e_at, e_put, h_ref, hz_ref, ci_at, q - 2, fn)
 
     even = reach + reach % 2
     own, end = GHOST, GHOST + NX
-    ranges = ((own - even - 2, own + 2, None), (own + 2, end + 2, use), (end + 2, GHOST + NX + reach - 1 + reach % 2 * 1 + 2, None))
-    ranges = ranges[:2] + ((end + 2, end + even + 2 if reach % 2 == 0 else end + reach + 1, None),)
+    last = end + even + 2 if reach % 2 == 0 else end + reach + 1
+    ranges = ((own - even - 2, own + 2, None), (own + 2, end + 2, use), (end + 2, last, None))
     for start, stop, fn in ranges:
         if stop > start:
             @pl.loop(0, (stop - start) // 2)
@@ -238,21 +242,66 @@
     return [pltpu.VMEM(x.shape, F32) for x in arrays] + [pltpu.SemaphoreType.DMA((len(arrays),))]
 
 
-def fill_inverse(perm_ref, ci_ref):
-    places = [(s, 0, GHOST + s) for s in range(NX)]
-    places += [(s, 1, GHOST + NX + s) for s in range(DEEP - 1)]
-    places += [(s, 1, s - NX + GHOST) for s in range(NX - DEEP + 1, NX)]
-    for s, which, place in places:
-        t = widen(perm_ref[s, which])
-        store(ci_ref, (place,), [jnp.where(x > 0, (courant * courant) / jnp.where(x > 0, x, 1.0), 0.0) for x in t])
-
-
-def adjoint_body(tile_ref, perm_ref, a_ref, b_ref, up_ref, dn_ref, hist_ref, ci_ref, h_ref, e_ref, ez_ref, hz_ref, sem, *staged):
+def fill_inverse(core, mine_ref, other_ref, ci_ref):
+    for ref, odd in ((mine_ref, core), (other_ref, 1 - core)):
+        for j in range(NX // 2):
+            places = [(0, GHOST)]
+            if 2 * j < DEEP - 1:
+                places.append((1, GHOST + NX))
+            if 2 * j + 1 > NX - DEEP:
+                places.append((1, GHOST - NX))
+            for which, base in places:
+                t = widen(ref[j, which])
+                t = [jnp.where(x > 0, (courant * courant) / jnp.where(x > 0, x, 1.0), 0.0) for x in t]
+                store(ci_ref, (base + 2 * j + odd,), t)
+
+
+def products(a, curl):
+    f = lambda x0, y0, x1, y1, x2, y2: x0 * y0 + x1 * y1 + x2 * y2
+    return joined(each(f, a[0], curl[0], a[1], curl[1], a[2], curl[2]))
+
+
+def interior_body(where_ref, mine_ref, other_ref, e0_ref, h0_ref, e_ref, h_ref, ci_ref, past_ref, ez_ref, hz_ref):
     sh = Shifts()
-    tile = tile_ref[0]
+    fill_inverse(where_ref[1], mine_ref, other_ref, ci_ref)
+    for c in range(3):
+        @pl.loop(0, NX)
+        def _(p):
+            store(e_ref, (c, p), widen(e0_ref[0, c, p]))
+            store(h_ref, (c, p), [x * (1.0 / courant) for x in widen(h0_ref[0, c, p])])
+
+    e_at = lambda c, p: e_ref[c, p]
+    ci_at = lambda p: ci_ref[p + GHOST]
+
+    def e_put(c, p, x):
+        e_ref[c, p] = x
+
+    def turn(t):
+        def use(p, curl):
+            for c in range(3):
+                past_ref[t, c, p] = joined(curl[c])
+
+        z_phase(sh, e_at, ez_ref, [t + k for k in range(5)])
+        h_phase(sh, e_at, h_ref, ez_ref, hz_ref, t, 1)
+        h_phase(sh, e_at, h_ref, ez_ref, hz_ref, t + 1)
+
+        @pl.loop(1, NX // 2 - 1 - t)
+        def _(i):
+            q = t + 1 + 2 * i
+            z_phase(sh, e_at, ez_ref, (q + 2, q + 3))
+            h_phase(sh, e_at, h_ref, ez_ref, hz_ref, q)
+            e_phase(sh, e_at, e_put, h_ref, hz_ref, ci_at, q - 2, use)
+
+        e_phase(sh, e_at, e_put, h_ref, hz_ref, ci_at, NX - 3 - t, use)
+
+    for t in range(STEPS):
+        turn(t)
+
+
+def adjoint_body(where_ref, ci_ref, a_ref, b_ref, up_ref, dn_ref, past_ref, e_ref, sum_ref, h_ref, ez_ref, hz_ref, *staged):
+    sh = Shifts()
     depth = STEPS - 1
     up_ref, dn_ref, ready = stage((up_ref, dn_ref), *staged)
-    fill_inverse(perm_ref, ci_ref)
 
     def put(a, c, place, t):
         if a == 1:
@@ -270,10 +319,6 @@
     unpack(depth, up_ref, True, put)
     unpack(depth, dn_ref, False, put)
 
-    def out(j):
-        return pltpu.make_async_copy(e_ref.at[j, :, pl.ds(GHOST, NX)], hist_ref.at[j], sem.at[j])
-
-    out(0).start()
     for j in range(depth):
         def e_put(c, p, x, j=j):
             e_ref[j + 1, c, p] = x
@@ -281,24 +326,25 @@
         def e_mirror(c, j=j):
             e_ref[j, c, GHOST - 1] = e_ref[j, c, GHOST]
 
-        sweep(sh, tile, depth - j, lambda c, p, j=j: e_ref[j, c, p], e_put, e_mirror, h_ref, ez_ref, hz_ref, ci_ref, None)
-        out(j + 1).start()
-    for j in range(depth + 1):
-        out(j).wait()
-
-
-def forward_body(tile_ref, perm_ref, e0_ref, h0_ref, up_ref, dn_ref, hist_ref, efin_ref, sum_ref, ci_ref, h_ref, e_ref, ahat_ref, ez_ref, hz_ref, sem, *staged):
+        sweep(sh, where_ref[0], depth - j, lambda c, p, j=j: e_ref[j, c, p], e_put, e_mirror, h_ref, ez_ref, hz_ref, lambda p: ci_ref[p], None)
+
+    for p in (0, NX - 1):
+        sum_ref[p] = jnp.zeros((NY, WIDE), F32)
+    for t in range(STEPS):
+        @pl.loop(0, NX // 2 - 1 - t)
+        def _(i, t=t):
+            for d in range(2):
+                p = t + 1 + 2 * i + d
+                s = products([tiles_of(e_ref[depth - t, c, p + GHOST]) for c in range(3)], [tiles_of(past_ref[t, c, p]) for c in range(3)])
+                sum_ref[p] = s + sum_ref[p] if t > 0 else s
+
+
+def forward_body(where_ref, ci_ref, e1_ref, h1_ref, part_ref, up_ref, dn_ref, hist_ref, efin_ref, sum_ref, h_ref, e_ref, acc_ref, ez_ref, hz_ref, *staged):
     sh = Shifts()
-    tile = tile_ref[0]
     depth = STEPS
-
-    def fetch(j):
-        return pltpu.make_async_copy(hist_ref.at[j], ahat_ref.at[j], sem.at[j])
+    edge = NX // 2 - 1
 
     up_ref, dn_ref, ready = stage((up_ref, dn_ref), *staged)
-    for t in range(STEPS):
-        fetch(STEPS - 1 - t).start()
-    fill_inverse(perm_ref, ci_ref)
 
     def put(a, c, place, t):
         if a == 1:
@@ -306,11 +352,18 @@
         else:
             store(e_ref, (c, place), t)
 
+    for start in (0, NX - edge):
+        @pl.loop(start, start + edge)
+        def _(p):
+            acc_ref[p + GHOST] = part_ref[p]
+            for c in range(3):
+                e_ref[c, p + GHOST] = e1_ref[c, p]
+                h_ref[c, p + GHOST] = h1_ref[c, p]
     for c in range(3):
-        @pl.loop(0, NX)
-        def _(p):
-            put(0, c, p + GHOST, widen(e0_ref[0, c, p]))
-            put(1, c, p + GHOST, widen(h0_ref[0, c, p]))
+        for p in range(DEEP, NX - DEEP):
+            efin_ref[0, c, p] = e1_ref[c, p][:, :NZ]
+    for p in range(DEEP, NX - DEEP):
+        sum_ref[p] = part_ref[p]
     ready(0, 1)
     unpack(depth, up_ref, True, put)
     unpack(depth, dn_ref, False, put)
@@ -319,86 +372,117 @@
     for c in (1, 2):
         e_ref[c, last] = e_ref[c, last + 1]
 
+    e_at = lambda c, p: e_ref[c, p]
+    ci_at = lambda p: ci_ref[p]
+
     def e_put(c, p, x):
         e_ref[c, p] = x
 
-    def e_mirror(c):
-        e_ref[c, GHOST - 1] = e_ref[c, GHOST]
-
-    for t in range(STEPS):
-        fetch(STEPS - 1 - t).wait()
-
-        def use(p, curl, t=t):
-            q = p - GHOST
-            a = [tiles_of(ahat_ref[STEPS - 1 - t, c, q]) for c in range(3)]
-            s = each(lambda x0, y0, x1, y1, x2, y2: x0 * y0 + x1 * y1 + x2 * y2, a[0], curl[0], a[1], curl[1], a[2], curl[2])
-            s = joined(s)
-            if t > 0:
-                s = s + sum_ref[q]
-            sum_ref[q] = s
-
-        sweep(sh, tile, depth - t, lambda c, p: e_ref[c, p], e_put, e_mirror, h_ref, ez_ref, hz_ref, ci_ref, use)
-    for c in range(3):
-        @pl.loop(0, NX)
+    @pl.loop(0, STEPS)
+    def _(t):
+        @pl.when(where_ref[0] == 0)
+        def _():
+            for c in (1, 2):
+                e_ref[c, GHOST - 1] = e_ref[c, GHOST]
+
+        def use(p, curl):
+            a = [tiles_of(hist_ref[STEPS - 1 - t, c, p]) for c in range(3)]
+            acc_ref[p] = acc_ref[p] + products(a, curl)
+
+        low, high = GHOST - DEEP + t, GHOST + NX - 1 - t
+        Z = lambda base, k: z_phase(sh, e_at, ez_ref, (base + 2 * k, base + 2 * k + 1))
+        H = lambda base, k: h_phase(sh, e_at, h_ref, ez_ref, hz_ref, base + 2 * k)
+        E = lambda base, k: e_phase(sh, e_at, e_put, h_ref, hz_ref, ci_at, base + 2 * k, use)
+        for c in range(2):
+            hz_ref[c, low + DEEP] = joined(sh.behind_z(tiles_of(h_ref[c, low + DEEP])))
+        Z(low, 0), Z(high, 0), Z(low, 1)
+        H(low, 0), Z(high, 1)
+        H(high, 0), Z(low, 2)
+        H(low, 1), Z(high, 2)
+        H(high, 1)
+        H(low, 2), E(low + 1, 0)
+        H(high, 2), E(high, 0)
+        E(low + 1, 1), E(high, 1)
+        E(low + 1, 2), E(high, 2)
+
+    for start in (0, NX - DEEP):
+        @pl.loop(start, start + DEEP)
         def _(p):
-            efin_ref[0, c, p] = e_ref[c, p + GHOST][:, :NZ]
+            sum_ref[p] = acc_ref[p + GHOST]
+            for c in range(3):
+                efin_ref[0, c, p] = e_ref[c, p + GHOST][:, :NZ]
 
 
 VM = pl.BlockSpec(memory_space=pltpu.VMEM)
 HBM = pl.BlockSpec(memory_space=pltpu.HBM)
 SM = pl.BlockSpec(memory_space=pltpu.SMEM)
 FIELD = (3, ALL, NY, WIDE)
-
-
-def adjoint(tile, perm, a, b, up, dn, interpret=False):
+PAIR = (2, ALL, NY, WIDE)
+ROOM = 18
+
+
+def shape(*sizes):
+    return jax.ShapeDtypeStruct(sizes, F32)
+
+
+def params(mib):
+    return pltpu.CompilerParams(vmem_limit_bytes=mib << 20)
+
+
+def interior(where, mine, other, e, h):
+    return pl.pallas_call(
+        interior_body,
+        out_shape=(shape(3, ROOM, NY, WIDE), shape(3, ROOM, NY, WIDE), shape(ALL, NY, WIDE), shape(STEPS, 3, NX, NY, WIDE)),
+        in_specs=[SM, VM, VM, VM, VM],
+        out_specs=(VM, VM, VM, VM),
+        scratch_shapes=[
+            pltpu.VMEM((2, ROOM, NY, WIDE), F32),
+            pltpu.VMEM((2, ROOM, NY, WIDE), F32),
+        ],
+        compiler_params=params(20),
+        name="interior",
+    )(where, mine, other, e, h)
+
+
+def adjoint(where, ci, a, b, up, dn, past):
     return pl.pallas_call(
         adjoint_body,
-        out_shape=jax.ShapeDtypeStruct((STEPS, 3, NX, NY, WIDE), F32),
-        in_specs=[SM, VM, VM, VM, HBM, HBM],
-        out_specs=HBM,
+        out_shape=(shape(STEPS, *FIELD), shape(NX, NY, WIDE)),
+        in_specs=[SM, VM, VM, VM, HBM, HBM, VM],
+        out_specs=(VM, VM),
         scratch_shapes=[
-            pltpu.VMEM((ALL, NY, WIDE), F32),
             pltpu.VMEM(FIELD, F32),
-            pltpu.VMEM((STEPS, *FIELD), F32),
-            pltpu.VMEM((2, ALL, NY, WIDE), F32),
-            pltpu.VMEM((2, ALL, NY, WIDE), F32),
-            pltpu.SemaphoreType.DMA((STEPS,)),
+            pltpu.VMEM(PAIR, F32),
+            pltpu.VMEM(PAIR, F32),
             *staging(up, dn),
         ],
-        compiler_params=pltpu.CompilerParams(vmem_limit_bytes=44 << 20),
+        compiler_params=params(18),
         name="adjoint",
-        interpret=interpret,
-    )(tile, perm, a, b, up, dn)
-
-
-def forward(tile, perm, e, h, up, dn, hist, interpret=False):
+    )(where, ci, a, b, up, dn, past)
+
+
+def forward(where, ci, e1, h1, part, up, dn, hist):
     return pl.pallas_call(
         forward_body,
-        out_shape=(
-            jax.ShapeDtypeStruct((1, 3, NX, NY, NZ), F32),
-            jax.ShapeDtypeStruct((NX, NY, WIDE), F32),
-        ),
-        in_specs=[SM, VM, VM, VM, HBM, HBM, HBM],
+        out_shape=(shape(1, 3, NX, NY, NZ), shape(NX, NY, WIDE)),
+        in_specs=[SM, VM, VM, VM, VM, HBM, HBM, VM],
         out_specs=(VM, VM),
         scratch_shapes=[
-            pltpu.VMEM((ALL, NY, WIDE), F32),
             pltpu.VMEM(FIELD, F32),
             pltpu.VMEM(FIELD, F32),
-            pltpu.VMEM((STEPS, 3, NX, NY, WIDE), F32),
-            pltpu.VMEM((2, ALL, NY, WIDE), F32),
-            pltpu.VMEM((2, ALL, NY, WIDE), F32),
-            pltpu.SemaphoreType.DMA((STEPS,)),
+            pltpu.VMEM((ALL, NY, WIDE), F32),
+            pltpu.VMEM(PAIR, F32),
+            pltpu.VMEM(PAIR, F32),
             *staging(up, dn),
         ],
-        compiler_params=pltpu.CompilerParams(vmem_limit_bytes=44 << 20),
+        compiler_params=params(18),
         name="forward",
-        interpret=interpret,
-    )(tile, perm, e, h, up, dn, hist)
+    )(where, ci, e1, h1, part, up, dn, hist)
 
 
 def on_device(permittivity, e_start, h_start, e_cotangent, h_cotangent):
     tiles, sources = lax.axis_size("tile"), lax.axis_size("src")
-    tile = lax.axis_index("tile").astype(jnp.int32).reshape(1)
+    where = jnp.stack([lax.axis_index("tile"), lax.axis_index("src") % 2]).astype(jnp.int32)
     upward = [(i, i + 1) for i in range(tiles - 1)]
     downward = [(i + 1, i) for i in range(tiles - 1)]
     near = [(t * sources + s, (t - 1) * sources + s) for t in range(1, tiles) for s in range(DEEP - 1)]
@@ -409,12 +493,16 @@
     a_up = lax.ppermute(a_up, "tile", upward)
     a_dn = lax.ppermute(a_dn, "tile", downward)
     both = jnp.concatenate([permittivity, border], axis=0)
-    perm = lax.all_to_all(jnp.broadcast_to(both, (sources, *both.shape)), "src", 0, 0, tiled=True)
+    groups = [list(range(k, sources, 2)) for k in range(2)]
+    both = jnp.broadcast_to(both, (sources // 2, *both.shape))
+    mine = lax.all_to_all(both, "src", 0, 0, tiled=True, axis_index_groups=groups)
     e_up, e_dn = pack(STEPS, e_start, h_start)
     e_up = lax.ppermute(e_up, "tile", upward)
     e_dn = lax.ppermute(e_dn, "tile", downward)
-    hist = adjoint(tile, perm, e_cotangent, h_cotangent, a_up, a_dn)
-    e_final, sums = forward(tile, perm, e_start, h_start, e_up, e_dn, hist)
+    other = lax.ppermute(mine, "src", [(s, s ^ 1) for s in range(sources)])
+    e1, h1, ci, past = interior(where, mine, other, e_start, h_start)
+    hist, part = adjoint(where, ci, e_cotangent, h_cotangent, a_up, a_dn, past)
+    e_final, sums = forward(where, ci, e1, h1, part, e_up, e_dn, hist)
     parts = lax.all_to_all(sums, "src", 0, 0, tiled=True)
     total = jnp.sum(parts, axis=0, keepdims=True)[:, :, :NZ]
     gradient = -(courant * courant) * total / permittivity

time: 97.9 us -> 82.5 us (0.84)
  waiting for transfers between devices: 30.9 us -> 13.9 us
  starting transfers between devices: 21 us -> 24.3 us
  blocking collectives: 13.2 us -> 12.1 us
    ppermute x1, waiting for transfers between devices: 30.9 us -> 10.5 us  [on_device(): a_dn = lax.ppermute(a_dn, 'tile', downward)]
    ppermute x1, starting transfers between devices: 1.92 us -> 7.15 us  [on_device(): e_up = lax.ppermute(e_up, 'tile', upward)]
    ppermute x1, starting transfers between devices: 3.92 us -> 1.92 us  [on_device(): e_dn = lax.ppermute(e_dn, 'tile', downward)]
    ppermute x0 -> x1, waiting for transfers between devices: none -> 1.77 us  [on_device(): other = lax.ppermute(mine, 'src', [(s, s ^ 1) for s in range(sources)])]
    all_to_all x1, waiting for transfers between devices: 0.01 us -> 1.65 us  [on_device(): lax.all_to_all(both, 'src', 0, 0, tiled=True, axis_index_groups=groups)]
    all_to_all x1, blocking collectives: 13.2 us -> 12.1 us  [on_device(): parts = lax.all_to_all(sums, 'src', 0, 0, tiled=True)]
    pallas_call x2 -> x3, Pallas kernels: 24.9 us -> 24.3 us  [the longest x1 10.7 us: adjoint(): pl.pallas_call(adjoint_body, out_shape=(shape(STEPS, *FIELD), shape(NX, N...]
  transfers between devices with their start and end apart: 6 -> 7, of which waited for: 1 -> 3; matrix products, arithmetic and copies ran while one was open for 1% -> 1% of each run, Pallas kernels for 16% -> 26%
where the time goes in v2:
time: 82.5 us; the launch traced here: 81.9 us
  Pallas kernels  29.3 us (36%)
  starting transfers between devices  24.3 us (29%)
  waiting for transfers between devices  13.9 us (17%)
  blocking collectives  12.1 us (15%)
    all_to_all x1, blocking collectives, on_device(): parts = lax.all_to_all(sums, 'src', 0, 0, tiled=True)  12.1 us
    pallas_call x1, Pallas kernels, adjoint(): pl.pallas_call(adjoint_body, out_shape=(shape(STEPS, *FIELD), shape(NX, N...  10.7 us
    ppermute x1, waiting for transfers between devices, on_device(): a_dn = lax.ppermute(a_dn, 'tile', downward)  10.5 us
    pallas_call x1, Pallas kernels, forward(): pl.pallas_call(forward_body, out_shape=(shape(1, 3, NX, NY, NZ), shape(NX...  8.44 us
    ppermute x1, starting transfers between devices, on_device(): a_up = lax.ppermute(a_up, 'tile', upward)  7.54 us
    ppermute x1, starting transfers between devices, on_device(): e_up = lax.ppermute(e_up, 'tile', upward)  7.15 us
    pallas_call x1, Pallas kernels, interior(): pl.pallas_call(interior_body, out_shape=(shape(3, ROOM, NY, WIDE), shape(...  5.15 us
    pallas_call x2, Pallas kernels, pack(): pl.pallas_call(lambda *refs: pack_body(depth, *refs), out_shape=(jax.Shap...  5.03 us
  transfers between devices with their start and end apart: 7, of which 3 were waited for; matrix products, arithmetic and copies ran while one was open for 1% of the time, Pallas kernels for 26%

profile of v2, /device:TPU:96, one launch (start us, length us, event | category | flops | bytes accessed | tf_op | source)
XLA Modules:
  0.0 81.9 jit_solution(17678791184493233567)
XLA Ops:
  0.6 2.3 %collective-permute-start = (f32[1,16,320]{2,1,0:T(8,128)}, f32[1,16,320]{2,1,0:T(8,128)S(1)}, u32[]{:S(2)}, u32[]{:S(2)}) collective-permute-start(f32[1,16,320]{2,1,0:T(8,128)} %param.5), channel_id=1, source_target_pairs={{16,0},{17,1},{18,2},{19,3},{20,4},{32,16},{33,17},{34,18},{35,19}... | collective-permute-start | bytes 61448 | tf_op jit(solution)/shard_map/ppermute | solution.py:491
  3.0 2.5 %shard_map.69 = (f32[16,5,16,128]{3,2,1,0:T(8,128)}, f32[16,5,16,128]{3,2,1,0:T(8,128)}) custom-call(f32[1,3,16,16,320]{4,3,2,1,0:T(8,128)} %refs_0_.3, f32[1,3,16,16,320]{4,3,2,1,0:T(8,128)} %refs_1_.3), custom_call_target="tpu_custom_call" | custom-call | tf_op jit(solution)/shard_map/pallas_call | solution.py:72
  5.5 7.1 %collective-permute-start.4 = (f32[16,5,16,128]{3,2,1,0:T(8,128)}, f32[16,5,16,128]{3,2,1,0:T(8,128)S(1)}, u32[]{:S(2)}, u32[]{:S(2)}) collective-permute-start(f32[16,5,16,128]{3,2,1,0:T(8,128)} %get-tuple-element.21), channel_id=1, source_target_pairs={{0,16},{16,32},{32,48},{48,64},{64,80},{80,96},{96,112},{1,17},{17... | collective-permute-start | bytes 1966088 | tf_op jit(solution)/shard_map/ppermute | solution.py:500
  12.6 1.9 %collective-permute-start.5 = (f32[16,5,16,128]{3,2,1,0:T(8,128)}, f32[16,5,16,128]{3,2,1,0:T(8,128)}, u32[]{:S(2)}, u32[]{:S(2)}) collective-permute-start(f32[16,5,16,128]{3,2,1,0:T(8,128)} %get-tuple-element.22), channel_id=1, source_target_pairs={{16,0},{32,16},{48,32},{64,48},{80,64},{96,80},{112,96},{17,1},{33... | collective-permute-start | bytes 1966088 | tf_op jit(solution)/shard_map/ppermute | solution.py:501
  14.6 0.0 collective-permute-done
  14.6 0.8 broadcast_in_dim.6
  15.4 3.5 %all-to-all-start = ((f32[8,2,16,320]{3,2,1,0:T(8,128)}), f32[8,2,16,320]{3,2,1,0:T(8,128)S(1)}, u32[]{:S(2)}, u32[]{:S(2)}) async-start(f32[8,2,16,320]{3,2,1,0:T(8,128)} %broadcast_in_dim.6), calls=%async_computation | async-start | bytes 786432 | tf_op jit(solution)/shard_map/all_to_all | solution.py:498
  18.8 0.0 copy-start.2
  18.9 0.0 copy-start.3
  18.9 2.5 %shard_map.68 = (f32[15,5,16,128]{3,2,1,0:T(8,128)}, f32[13,5,16,128]{3,2,1,0:T(8,128)}) custom-call(f32[1,3,16,16,320]{4,3,2,1,0:T(8,128)} %a_ref.1, f32[1,3,16,16,320]{4,3,2,1,0:T(8,128)} %b_ref.1), custom_call_target="tpu_custom_call" | custom-call | tf_op jit(solution)/shard_map/pallas_call | solution.py:72
  21.4 7.5 %collective-permute-start.2 = (f32[15,5,16,128]{3,2,1,0:T(8,128)}, f32[15,5,16,128]{3,2,1,0:T(8,128)}, u32[]{:S(2)}, u32[]{:S(2)}) collective-permute-start(f32[15,5,16,128]{3,2,1,0:T(8,128)} %get-tuple-element.17), channel_id=1, source_target_pairs={{0,16},{16,32},{32,48},{48,64},{64,80},{80,96},{96,112},{1,17},{17... | collective-permute-start | bytes 1843208 | tf_op jit(solution)/shard_map/ppermute | solution.py:493
  28.9 1.9 %collective-permute-start.3 = (f32[13,5,16,128]{3,2,1,0:T(8,128)}, f32[13,5,16,128]{3,2,1,0:T(8,128)}, u32[]{:S(2)}, u32[]{:S(2)}) collective-permute-start(f32[13,5,16,128]{3,2,1,0:T(8,128)} %get-tuple-element.18), channel_id=1, source_target_pairs={{16,0},{32,16},{48,32},{64,48},{80,64},{96,80},{112,96},{17,1},{33... | collective-permute-start | bytes 1597448 | tf_op jit(solution)/shard_map/ppermute | solution.py:494
  30.9 1.7 %all-to-all-done.mine_ref = f32[8,2,16,320]{3,2,1,0:T(8,128)S(1)} async-done(((f32[8,2,16,320]{3,2,1,0:T(8,128)}), f32[8,2,16,320]{3,2,1,0:T(8,128)S(1)}, u32[]{:S(2)}, u32[]{:S(2)}) %all-to-all-start) | async-done | bytes 327712 | tf_op jit(solution)/shard_map/all_to_all | solution.py:498
  32.5 0.0 collective-permute-start.1
  32.5 0.1 pad_add_fusion.where_ref
  32.6 1.8 %collective-permute-done.1.other_ref = f32[8,2,16,320]{3,2,1,0:T(8,128)} collective-permute-done((f32[8,2,16,320]{3,2,1,0:T(8,128)S(1)}, f32[8,2,16,320]{3,2,1,0:T(8,128)}, u32[]{:S(2)}, u32[]{:S(2)}) %collective-permute-start.1) | collective-permute-done | bytes 327712 | tf_op jit(solution)/shard_map/ppermute | solution.py:502
  34.4 5.1 %interior.1 = (f32[3,18,16,384]{3,2,1,0:T(8,128)S(1)}, f32[3,18,16,384]{3,2,1,0:T(8,128)S(1)}, f32[40,16,384]{2,1,0:T(8,128)S(1)}, f32[6,3,16,16,384]{4,3,2,1,0:T(8,128)S(1)}) custom-call(s32[2]{0:T(128)S(1)} %pad_add_fusion.where_ref, f32[8,2,16,320]{3,2,1,0:T(8,128)S(1)} %all-to-all-done.mine_ref, f32[8,2,16,320]{3,2,1,0:T(8,128)} %collective-permute-done.1.other_ref, ...), custom_call_target="tpu_custom_call" | custom-call | tf_op jit(solution)/shard_map/interior/pallas_call | solution.py:433
  39.5 10.5 %collective-permute-done.3.dn_ref = f32[13,5,16,128]{3,2,1,0:T(8,128)} collective-permute-done((f32[13,5,16,128]{3,2,1,0:T(8,128)}, f32[13,5,16,128]{3,2,1,0:T(8,128)}, u32[]{:S(2)}, u32[]{:S(2)}) %collective-permute-start.3) | collective-permute-done | bytes 532512 | tf_op jit(solution)/shard_map/ppermute | solution.py:494
  50.0 10.7 %adjoint.1 = (f32[6,3,40,16,384]{4,3,2,1,0:T(8,128)S(1)}, f32[16,16,384]{2,1,0:T(8,128)S(1)}) custom-call(s32[2]{0:T(128)S(1)} %pad_add_fusion.where_ref, f32[40,16,384]{2,1,0:T(8,128)S(1)} %get-tuple-element.14.ci_ref, f32[1,3,16,16,320]{4,3,2,1,0:T(8,128)S(1)} %copy-done, f32[1,3,16,16,320]{4,3,2,1,0:T(8,128)S(1)} %copy-done.1, ...), custom_call_target="tpu_custom_call" | custom-call | tf_op jit(solution)/shard_map/adjoint/pallas_call | solution.py:448
  60.7 0.0 collective-permute-done.4.up_ref
  60.7 0.0 collective-permute-done.5.dn_ref
  60.8 8.4 %forward.1 = (f32[1,3,16,16,320]{4,3,2,1,0:T(8,128)}, f32[16,16,384]{2,1,0:T(8,128)S(1)}) custom-call(s32[2]{0:T(128)S(1)} %pad_add_fusion.where_ref, f32[40,16,384]{2,1,0:T(8,128)S(1)} %get-tuple-element.14.ci_ref, f32[3,18,16,384]{3,2,1,0:T(8,128)S(1)} %get-tuple-element.15.e1_ref, f32[3,18,16,384]{3,2,1,0:T(8,128)S(1)} %get-tuple-element.16.h1_ref, ...), custom_call_target="tpu_custom_call" | custom-call | tf_op jit(solution)/shard_map/forward/pallas_call | solution.py:465
  69.2 12.1 %all_to_all.10 = f32[16,16,384]{2,1,0:T(8,128)S(1)} all-to-all(f32[16,16,384]{2,1,0:T(8,128)S(1)} %get-tuple-element.25), channel_id=1, replica_groups=mesh['tile'=8,'src'=16] {'src'}, dimensions={0} | all-to-all | bytes 786432 | tf_op jit(solution)/shard_map/all_to_all | solution.py:506
  81.3 0.6 fusion
  (11 shorter events, 0.1 us)
Async XLA Ops:
  0.6 13.9 %copy-start.4 = (f32[1,16,320]{2,1,0:T(8,128)S(1)}, f32[1,16,320]{2,1,0:T(8,128)}, u32[]{:S(2)}) copy-start(f32[1,16,320]{2,1,0:T(8,128)} %param.5) | copy-start | bytes 61444
  0.6 13.9 %collective-permute-start = (f32[1,16,320]{2,1,0:T(8,128)}, f32[1,16,320]{2,1,0:T(8,128)S(1)}, u32[]{:S(2)}, u32[]{:S(2)}) collective-permute-start(f32[1,16,320]{2,1,0:T(8,128)} %param.5), channel_id=1, source_target_pairs={{16,0},{17,1},{18,2},{19,3},{20,4},{32,16},{33,17},{34,18},{35,19}... | collective-permute-start | bytes 61448 | tf_op jit(solution)/shard_map/ppermute | solution.py:491
  5.5 55.3 %collective-permute-start.4 = (f32[16,5,16,128]{3,2,1,0:T(8,128)}, f32[16,5,16,128]{3,2,1,0:T(8,128)S(1)}, u32[]{:S(2)}, u32[]{:S(2)}) collective-permute-start(f32[16,5,16,128]{3,2,1,0:T(8,128)} %get-tuple-element.21), channel_id=1, source_target_pairs={{0,16},{16,32},{32,48},{48,64},{64,80},{80,96},{96,112},{1,17},{17... | collective-permute-start | bytes 1966088 | tf_op jit(solution)/shard_map/ppermute | solution.py:500
  12.6 48.1 %collective-permute-start.5 = (f32[16,5,16,128]{3,2,1,0:T(8,128)}, f32[16,5,16,128]{3,2,1,0:T(8,128)}, u32[]{:S(2)}, u32[]{:S(2)}) collective-permute-start(f32[16,5,16,128]{3,2,1,0:T(8,128)} %get-tuple-element.22), channel_id=1, source_target_pairs={{16,0},{32,16},{48,32},{64,48},{80,64},{96,80},{112,96},{17,1},{33... | collective-permute-start | bytes 1966088 | tf_op jit(solution)/shard_map/ppermute | solution.py:501
  15.4 17.1 %all-to-all-start = ((f32[8,2,16,320]{3,2,1,0:T(8,128)}), f32[8,2,16,320]{3,2,1,0:T(8,128)S(1)}, u32[]{:S(2)}, u32[]{:S(2)}) async-start(f32[8,2,16,320]{3,2,1,0:T(8,128)} %broadcast_in_dim.6), calls=%async_computation | async-start | bytes 786432 | tf_op jit(solution)/shard_map/all_to_all | solution.py:498
  18.8 15.5 %copy-start.2 = (f32[1,3,16,16,320]{4,3,2,1,0:T(8,128)S(1)}, f32[1,3,16,16,320]{4,3,2,1,0:T(8,128)}, u32[]{:S(2)}) copy-start(f32[1,3,16,16,320]{4,3,2,1,0:T(8,128)} %refs_0_.3) | copy-start | bytes 2949124
  18.9 15.5 %copy-start.3 = (f32[1,3,16,16,320]{4,3,2,1,0:T(8,128)S(1)}, f32[1,3,16,16,320]{4,3,2,1,0:T(8,128)}, u32[]{:S(2)}) copy-start(f32[1,3,16,16,320]{4,3,2,1,0:T(8,128)} %refs_1_.3) | copy-start | bytes 2949124
  21.4 28.6 %collective-permute-start.2 = (f32[15,5,16,128]{3,2,1,0:T(8,128)}, f32[15,5,16,128]{3,2,1,0:T(8,128)}, u32[]{:S(2)}, u32[]{:S(2)}) collective-permute-start(f32[15,5,16,128]{3,2,1,0:T(8,128)} %get-tuple-element.17), channel_id=1, source_target_pairs={{0,16},{16,32},{32,48},{48,64},{64,80},{80,96},{96,112},{1,17},{17... | collective-permute-start | bytes 1843208 | tf_op jit(solution)/shard_map/ppermute | solution.py:493
  28.9 21.1 %collective-permute-start.3 = (f32[13,5,16,128]{3,2,1,0:T(8,128)}, f32[13,5,16,128]{3,2,1,0:T(8,128)}, u32[]{:S(2)}, u32[]{:S(2)}) collective-permute-start(f32[13,5,16,128]{3,2,1,0:T(8,128)} %get-tuple-element.18), channel_id=1, source_target_pairs={{16,0},{32,16},{48,32},{64,48},{80,64},{96,80},{112,96},{17,1},{33... | collective-permute-start | bytes 1597448 | tf_op jit(solution)/shard_map/ppermute | solution.py:494
  32.5 1.9 %collective-permute-start.1 = (f32[8,2,16,320]{3,2,1,0:T(8,128)S(1)}, f32[8,2,16,320]{3,2,1,0:T(8,128)}, u32[]{:S(2)}, u32[]{:S(2)}) collective-permute-start(f32[8,2,16,320]{3,2,1,0:T(8,128)S(1)} %all-to-all-done.mine_ref), channel_id=1, source_target_pairs={{0,1},{1,0},{2,3},{3,2},{4,5},{5,4},{6,7},{7,6},{8,9},{9,8},{10,11... | collective-permute-start | bytes 983048 | tf_op jit(solution)/shard_map/ppermute | solution.py:502
  32.6 17.4 %copy-start = (f32[1,3,16,16,320]{4,3,2,1,0:T(8,128)S(1)}, f32[1,3,16,16,320]{4,3,2,1,0:T(8,128)}, u32[]{:S(2)}) copy-start(f32[1,3,16,16,320]{4,3,2,1,0:T(8,128)} %a_ref.1) | copy-start | bytes 2949124
  32.6 17.4 %copy-start.1 = (f32[1,3,16,16,320]{4,3,2,1,0:T(8,128)S(1)}, f32[1,3,16,16,320]{4,3,2,1,0:T(8,128)}, u32[]{:S(2)}) copy-start(f32[1,3,16,16,320]{4,3,2,1,0:T(8,128)} %b_ref.1) | copy-start | bytes 2949124

commit v3 on v2

--- a/solution.py
+++ b/solution.py
@@ -204,26 +204,23 @@
         before = h
 
 
-def sweep(sh, tile, reach, e_at, e_put, e_mirror, h_ref, ez_ref, hz_ref, ci_at, use):
-    @pl.when(tile == 0)
-    def _():
-        for c in (1, 2):
-            e_mirror(c)
-
-    def turn(q, fn):
+def sweep(sh, first, reach, e_at, e_put, e_mirror, h_ref, ez_ref, hz_ref, ci_at, use):
+    for c in (1, 2):
+        e_mirror(c, jnp.where(first, e_at(c, GHOST), e_at(c, GHOST - 1)))
+    low = GHOST - reach
+    pairs = NX // 2 - 1 + reach
+    z_phase(sh, e_at, ez_ref, range(low, low + 5))
+    h_phase(sh, e_at, h_ref, ez_ref, hz_ref, low, 1)
+    h_phase(sh, e_at, h_ref, ez_ref, hz_ref, low + 1)
+
+    @pl.loop(1, pairs)
+    def _(i):
+        q = low + 1 + 2 * i
         z_phase(sh, e_at, ez_ref, (q + 2, q + 3))
         h_phase(sh, e_at, h_ref, ez_ref, hz_ref, q)
-        e_phase(sh, e_at, e_put, h_ref, hz_ref, ci_at, q - 2, fn)
-
-    even = reach + reach % 2
-    own, end = GHOST, GHOST + NX
-    last = end + even + 2 if reach % 2 == 0 else end + reach + 1
-    ranges = ((own - even - 2, own + 2, None), (own + 2, end + 2, use), (end + 2, last, None))
-    for start, stop, fn in ranges:
-        if stop > start:
-            @pl.loop(0, (stop - start) // 2)
-            def _(i, start=start, fn=fn):
-                turn(start + 2 * i, fn)
+        e_phase(sh, e_at, e_put, h_ref, hz_ref, ci_at, q - 2, use)
+
+    e_phase(sh, e_at, e_put, h_ref, hz_ref, ci_at, low - 1 + 2 * pairs, use)
 
 
 def stage(refs, *staged):
@@ -261,47 +258,11 @@
     return joined(each(f, a[0], curl[0], a[1], curl[1], a[2], curl[2]))
 
 
-def interior_body(where_ref, mine_ref, other_ref, e0_ref, h0_ref, e_ref, h_ref, ci_ref, past_ref, ez_ref, hz_ref):
-    sh = Shifts()
-    fill_inverse(where_ref[1], mine_ref, other_ref, ci_ref)
-    for c in range(3):
-        @pl.loop(0, NX)
-        def _(p):
-            store(e_ref, (c, p), widen(e0_ref[0, c, p]))
-            store(h_ref, (c, p), [x * (1.0 / courant) for x in widen(h0_ref[0, c, p])])
-
-    e_at = lambda c, p: e_ref[c, p]
-    ci_at = lambda p: ci_ref[p + GHOST]
-
-    def e_put(c, p, x):
-        e_ref[c, p] = x
-
-    def turn(t):
-        def use(p, curl):
-            for c in range(3):
-                past_ref[t, c, p] = joined(curl[c])
-
-        z_phase(sh, e_at, ez_ref, [t + k for k in range(5)])
-        h_phase(sh, e_at, h_ref, ez_ref, hz_ref, t, 1)
-        h_phase(sh, e_at, h_ref, ez_ref, hz_ref, t + 1)
-
-        @pl.loop(1, NX // 2 - 1 - t)
-        def _(i):
-            q = t + 1 + 2 * i
-            z_phase(sh, e_at, ez_ref, (q + 2, q + 3))
-            h_phase(sh, e_at, h_ref, ez_ref, hz_ref, q)
-            e_phase(sh, e_at, e_put, h_ref, hz_ref, ci_at, q - 2, use)
-
-        e_phase(sh, e_at, e_put, h_ref, hz_ref, ci_at, NX - 3 - t, use)
-
-    for t in range(STEPS):
-        turn(t)
-
-
-def adjoint_body(where_ref, ci_ref, a_ref, b_ref, up_ref, dn_ref, past_ref, e_ref, sum_ref, h_ref, ez_ref, hz_ref, *staged):
+def adjoint_body(where_ref, mine_ref, other_ref, a_ref, b_ref, up_ref, dn_ref, e_ref, ci_ref, h_ref, ez_ref, hz_ref, *staged):
     sh = Shifts()
     depth = STEPS - 1
     up_ref, dn_ref, ready = stage((up_ref, dn_ref), *staged)
+    fill_inverse(where_ref[1], mine_ref, other_ref, ci_ref)
 
     def put(a, c, place, t):
         if a == 1:
@@ -310,40 +271,28 @@
             ci = ci_ref[place]
             store(e_ref, (0, c, place), [t[k] * ci[:, 128 * k : 128 * k + 128] * (1.0 / (courant * courant)) for k in range(3)])
 
-    for c in range(3):
-        @pl.loop(0, NX)
-        def _(p):
+    @pl.loop(0, NX)
+    def _(p):
+        for c in range(3):
             put(0, c, p + GHOST, widen(a_ref[0, c, p]))
             put(1, c, p + GHOST, widen(b_ref[0, c, p]))
+
     ready(0, 1)
     unpack(depth, up_ref, True, put)
     unpack(depth, dn_ref, False, put)
-
     for j in range(depth):
         def e_put(c, p, x, j=j):
             e_ref[j + 1, c, p] = x
 
-        def e_mirror(c, j=j):
-            e_ref[j, c, GHOST - 1] = e_ref[j, c, GHOST]
-
-        sweep(sh, where_ref[0], depth - j, lambda c, p, j=j: e_ref[j, c, p], e_put, e_mirror, h_ref, ez_ref, hz_ref, lambda p: ci_ref[p], None)
-
-    for p in (0, NX - 1):
-        sum_ref[p] = jnp.zeros((NY, WIDE), F32)
-    for t in range(STEPS):
-        @pl.loop(0, NX // 2 - 1 - t)
-        def _(i, t=t):
-            for d in range(2):
-                p = t + 1 + 2 * i + d
-                s = products([tiles_of(e_ref[depth - t, c, p + GHOST]) for c in range(3)], [tiles_of(past_ref[t, c, p]) for c in range(3)])
-                sum_ref[p] = s + sum_ref[p] if t > 0 else s
-
-
-def forward_body(where_ref, ci_ref, e1_ref, h1_ref, part_ref, up_ref, dn_ref, hist_ref, efin_ref, sum_ref, h_ref, e_ref, acc_ref, ez_ref, hz_ref, *staged):
+        def e_mirror(c, x, j=j):
+            e_ref[j, c, GHOST - 1] = x
+
+        sweep(sh, where_ref[0] == 0, depth - j, lambda c, p, j=j: e_ref[j, c, p], e_put, e_mirror, h_ref, ez_ref, hz_ref, lambda p: ci_ref[p], None)
+
+
+def forward_body(where_ref, ci_ref, e0_ref, h0_ref, up_ref, dn_ref, hist_ref, efin_ref, sum_ref, h_ref, e_ref, acc_ref, ez_ref, hz_ref, *staged):
     sh = Shifts()
     depth = STEPS
-    edge = NX // 2 - 1
-
     up_ref, dn_ref, ready = stage((up_ref, dn_ref), *staged)
 
     def put(a, c, place, t):
@@ -352,18 +301,12 @@
         else:
             store(e_ref, (c, place), t)
 
-    for start in (0, NX - edge):
-        @pl.loop(start, start + edge)
-        def _(p):
-            acc_ref[p + GHOST] = part_ref[p]
-            for c in range(3):
-                e_ref[c, p + GHOST] = e1_ref[c, p]
-                h_ref[c, p + GHOST] = h1_ref[c, p]
-    for c in range(3):
-        for p in range(DEEP, NX - DEEP):
-            efin_ref[0, c, p] = e1_ref[c, p][:, :NZ]
-    for p in range(DEEP, NX - DEEP):
-        sum_ref[p] = part_ref[p]
+    @pl.loop(0, NX)
+    def _(p):
+        for c in range(3):
+            put(0, c, p + GHOST, widen(e0_ref[0, c, p]))
+            put(1, c, p + GHOST, widen(h0_ref[0, c, p]))
+
     ready(0, 1)
     unpack(depth, up_ref, True, put)
     unpack(depth, dn_ref, False, put)
@@ -372,45 +315,28 @@
     for c in (1, 2):
         e_ref[c, last] = e_ref[c, last + 1]
 
-    e_at = lambda c, p: e_ref[c, p]
-    ci_at = lambda p: ci_ref[p]
-
-    def e_put(c, p, x):
-        e_ref[c, p] = x
-
-    @pl.loop(0, STEPS)
-    def _(t):
-        @pl.when(where_ref[0] == 0)
-        def _():
-            for c in (1, 2):
-                e_ref[c, GHOST - 1] = e_ref[c, GHOST]
-
-        def use(p, curl):
-            a = [tiles_of(hist_ref[STEPS - 1 - t, c, p]) for c in range(3)]
-            acc_ref[p] = acc_ref[p] + products(a, curl)
-
-        low, high = GHOST - DEEP + t, GHOST + NX - 1 - t
-        Z = lambda base, k: z_phase(sh, e_at, ez_ref, (base + 2 * k, base + 2 * k + 1))
-        H = lambda base, k: h_phase(sh, e_at, h_ref, ez_ref, hz_ref, base + 2 * k)
-        E = lambda base, k: e_phase(sh, e_at, e_put, h_ref, hz_ref, ci_at, base + 2 * k, use)
-        for c in range(2):
-            hz_ref[c, low + DEEP] = joined(sh.behind_z(tiles_of(h_ref[c, low + DEEP])))
-        Z(low, 0), Z(high, 0), Z(low, 1)
-        H(low, 0), Z(high, 1)
-        H(high, 0), Z(low, 2)
-        H(low, 1), Z(high, 2)
-        H(high, 1)
-        H(low, 2), E(low + 1, 0)
-        H(high, 2), E(high, 0)
-        E(low + 1, 1), E(high, 1)
-        E(low + 1, 2), E(high, 2)
-
-    for start in (0, NX - DEEP):
-        @pl.loop(start, start + DEEP)
-        def _(p):
-            sum_ref[p] = acc_ref[p + GHOST]
-            for c in range(3):
-                efin_ref[0, c, p] = e_ref[c, p + GHOST][:, :NZ]
+    def e_mirror(c, x):
+        e_ref[c, GHOST - 1] = x
+
+    for t in range(STEPS):
+        done = t == STEPS - 1
+
+        def e_put(c, p, x, done=done):
+            if done:
+                efin_ref[0, c, p - GHOST] = x[:, :NZ]
+            else:
+                e_ref[c, p] = x
+
+        def use(p, curl, t=t, done=done):
+            s = products([tiles_of(hist_ref[STEPS - 1 - t, c, p]) for c in range(3)], curl)
+            if t > 0:
+                s = s + acc_ref[p]
+            if done:
+                sum_ref[p - GHOST] = s
+            else:
+                acc_ref[p] = s
+
+        sweep(sh, where_ref[0] == 0, depth - t, lambda c, p: e_ref[c, p], e_put, e_mirror, h_ref, ez_ref, hz_ref, lambda p: ci_ref[p], use)
 
 
 VM = pl.BlockSpec(memory_space=pltpu.VMEM)
@@ -418,7 +344,6 @@
 SM = pl.BlockSpec(memory_space=pltpu.SMEM)
 FIELD = (3, ALL, NY, WIDE)
 PAIR = (2, ALL, NY, WIDE)
-ROOM = 18
 
 
 def shape(*sizes):
@@ -429,26 +354,11 @@
     return pltpu.CompilerParams(vmem_limit_bytes=mib << 20)
 
 
-def interior(where, mine, other, e, h):
-    return pl.pallas_call(
-        interior_body,
-        out_shape=(shape(3, ROOM, NY, WIDE), shape(3, ROOM, NY, WIDE), shape(ALL, NY, WIDE), shape(STEPS, 3, NX, NY, WIDE)),
-        in_specs=[SM, VM, VM, VM, VM],
-        out_specs=(VM, VM, VM, VM),
-        scratch_shapes=[
-            pltpu.VMEM((2, ROOM, NY, WIDE), F32),
-            pltpu.VMEM((2, ROOM, NY, WIDE), F32),
-        ],
-        compiler_params=params(20),
-        name="interior",
-    )(where, mine, other, e, h)
-
-
-def adjoint(where, ci, a, b, up, dn, past):
+def adjoint(where, mine, other, a, b, up, dn):
     return pl.pallas_call(
         adjoint_body,
-        out_shape=(shape(STEPS, *FIELD), shape(NX, NY, WIDE)),
-        in_specs=[SM, VM, VM, VM, HBM, HBM, VM],
+        out_shape=(shape(STEPS, *FIELD), shape(ALL, NY, WIDE)),
+        in_specs=[SM, VM, VM, VM, VM, HBM, HBM],
         out_specs=(VM, VM),
         scratch_shapes=[
             pltpu.VMEM(FIELD, F32),
@@ -456,16 +366,16 @@
             pltpu.VMEM(PAIR, F32),
             *staging(up, dn),
         ],
-        compiler_params=params(18),
+        compiler_params=params(16),
         name="adjoint",
-    )(where, ci, a, b, up, dn, past)
-
-
-def forward(where, ci, e1, h1, part, up, dn, hist):
+    )(where, mine, other, a, b, up, dn)
+
+
+def forward(where, ci, e, h, up, dn, hist):
     return pl.pallas_call(
         forward_body,
         out_shape=(shape(1, 3, NX, NY, NZ), shape(NX, NY, WIDE)),
-        in_specs=[SM, VM, VM, VM, VM, HBM, HBM, VM],
+        in_specs=[SM, VM, VM, VM, HBM, HBM, VM],
         out_specs=(VM, VM),
         scratch_shapes=[
             pltpu.VMEM(FIELD, F32),
@@ -475,9 +385,9 @@
             pltpu.VMEM(PAIR, F32),
             *staging(up, dn),
         ],
-        compiler_params=params(18),
+        compiler_params=params(20),
         name="forward",
-    )(where, ci, e1, h1, part, up, dn, hist)
+    )(where, ci, e, h, up, dn, hist)
 
 
 def on_device(permittivity, e_start, h_start, e_cotangent, h_cotangent):
@@ -500,9 +410,8 @@
     e_up = lax.ppermute(e_up, "tile", upward)
     e_dn = lax.ppermute(e_dn, "tile", downward)
     other = lax.ppermute(mine, "src", [(s, s ^ 1) for s in range(sources)])
-    e1, h1, ci, past = interior(where, mine, other, e_start, h_start)
-    hist, part = adjoint(where, ci, e_cotangent, h_cotangent, a_up, a_dn, past)
-    e_final, sums = forward(where, ci, e1, h1, part, e_up, e_dn, hist)
+    hist, ci = adjoint(where, mine, other, e_cotangent, h_cotangent, a_up, a_dn)
+    e_final, sums = forward(where, ci, e_start, h_start, e_up, e_dn, hist)
     parts = lax.all_to_all(sums, "src", 0, 0, tiled=True)
     total = jnp.sum(parts, axis=0, keepdims=True)[:, :, :NZ]
     gradient = -(courant * courant) * total / permittivity

time: 82.5 us -> 89.1 us (1.080)
  waiting for transfers between devices: 13.9 us -> 27.2 us
  Pallas kernels: 29.3 us -> 25.1 us
  starting transfers between devices: 24.3 us -> 20.8 us
  blocking collectives: 12.1 us -> 13.2 us
    all_to_all x1, waiting for transfers between devices: 1.65 us -> 17.9 us  [on_device(): lax.all_to_all(both, 'src', 0, 0, tiled=True, axis_index_groups=groups)]
    pallas_call x2 -> x1, Pallas kernels: 15.9 us -> 9.04 us  [adjoint(): pl.pallas_call(adjoint_body, out_shape=(shape(STEPS, *FIELD), shape(ALL,...]
    ppermute x1, starting transfers between devices: 7.15 us -> 2.05 us  [on_device(): e_up = lax.ppermute(e_up, 'tile', upward)]
    pallas_call x1, Pallas kernels: 8.44 us -> 11.1 us  [forward(): pl.pallas_call(forward_body, out_shape=(shape(1, 3, NX, NY, NZ), shape(NX...]
    ppermute x1, starting transfers between devices: 1.92 us -> 3.92 us  [on_device(): e_dn = lax.ppermute(e_dn, 'tile', downward)]
    ppermute x1, waiting for transfers between devices: 1.77 us -> 0.01 us  [on_device(): other = lax.ppermute(mine, 'src', [(s, s ^ 1) for s in range(sources)])]
    ppermute x1, waiting for transfers between devices: 10.5 us -> 9.26 us  [on_device(): a_dn = lax.ppermute(a_dn, 'tile', downward)]
    all_to_all x1, blocking collectives: 12.1 us -> 13.2 us  [on_device(): parts = lax.all_to_all(sums, 'src', 0, 0, tiled=True)]
  transfers between devices with their start and end apart: 7 -> 7, of which waited for: 3 -> 2; matrix products, arithmetic and copies ran while one was open for 1% -> 1% of each run, Pallas kernels for 26% -> 16%
where the time goes in v3:
time: 89.1 us; the launch traced here: 88.6 us
  waiting for transfers between devices  27.2 us (31%)
  Pallas kernels  25.1 us (28%)
  starting transfers between devices  20.8 us (23%)
  blocking collectives  13.2 us (15%)
    all_to_all x1, waiting for transfers between devices, on_device(): lax.all_to_all(both, 'src', 0, 0, tiled=True, axis_index_groups=groups)  17.9 us
    all_to_all x1, blocking collectives, on_device(): parts = lax.all_to_all(sums, 'src', 0, 0, tiled=True)  13.2 us
    pallas_call x1, Pallas kernels, forward(): pl.pallas_call(forward_body, out_shape=(shape(1, 3, NX, NY, NZ), shape(NX...  11.1 us
    ppermute x1, waiting for transfers between devices, on_device(): a_dn = lax.ppermute(a_dn, 'tile', downward)  9.26 us
    pallas_call x1, Pallas kernels, adjoint(): pl.pallas_call(adjoint_body, out_shape=(shape(STEPS, *FIELD), shape(ALL,...  9.04 us
    ppermute x1, starting transfers between devices, on_device(): a_up = lax.ppermute(a_up, 'tile', upward)  7.15 us
    pallas_call x2, Pallas kernels, pack(): pl.pallas_call(lambda *refs: pack_body(depth, *refs), out_shape=(jax.Shap...  4.98 us
    ppermute x1, starting transfers between devices, on_device(): e_dn = lax.ppermute(e_dn, 'tile', downward)  3.92 us
  transfers between devices with their start and end apart: 7, of which 2 were waited for; matrix products, arithmetic and copies ran while one was open for 1% of the time, Pallas kernels for 16%

profile of v3, /device:TPU:96, one launch (start us, length us, event | category | flops | bytes accessed | tf_op | source)
XLA Modules:
  0.0 88.6 jit_solution(1224209236342413284)
XLA Ops:
  0.6 2.3 %collective-permute-start = (f32[1,16,320]{2,1,0:T(8,128)}, f32[1,16,320]{2,1,0:T(8,128)S(1)}, u32[]{:S(2)}, u32[]{:S(2)}) collective-permute-start(f32[1,16,320]{2,1,0:T(8,128)} %param.5), channel_id=1, source_target_pairs={{16,0},{17,1},{18,2},{19,3},{20,4},{32,16},{33,17},{34,18},{35,19}... | collective-permute-start | bytes 61448 | tf_op jit(solution)/shard_map/ppermute | solution.py:401
  2.9 2.4 %shard_map.68 = (f32[15,5,16,128]{3,2,1,0:T(8,128)}, f32[13,5,16,128]{3,2,1,0:T(8,128)}) custom-call(f32[1,3,16,16,320]{4,3,2,1,0:T(8,128)} %a_ref.1, f32[1,3,16,16,320]{4,3,2,1,0:T(8,128)} %b_ref.1), custom_call_target="tpu_custom_call" | custom-call | tf_op jit(solution)/shard_map/pallas_call | solution.py:72
  5.3 0.0 copy-start.4
  5.3 7.1 %collective-permute-start.2 = (f32[15,5,16,128]{3,2,1,0:T(8,128)}, f32[15,5,16,128]{3,2,1,0:T(8,128)}, u32[]{:S(2)}, u32[]{:S(2)}) collective-permute-start(f32[15,5,16,128]{3,2,1,0:T(8,128)} %get-tuple-element.10), channel_id=1, source_target_pairs={{0,16},{16,32},{32,48},{48,64},{64,80},{80,96},{96,112},{1,17},{17... | collective-permute-start | bytes 1843208 | tf_op jit(solution)/shard_map/ppermute | solution.py:403
  12.5 0.0 copy-start.3
  12.5 2.6 %shard_map.69 = (f32[16,5,16,128]{3,2,1,0:T(8,128)}, f32[16,5,16,128]{3,2,1,0:T(8,128)}) custom-call(f32[1,3,16,16,320]{4,3,2,1,0:T(8,128)} %e0_ref.1, f32[1,3,16,16,320]{4,3,2,1,0:T(8,128)} %h0_ref.1), custom_call_target="tpu_custom_call" | custom-call | tf_op jit(solution)/shard_map/pallas_call | solution.py:72
  15.1 0.0 copy-start.2
  15.1 2.1 %collective-permute-start.4 = (f32[16,5,16,128]{3,2,1,0:T(8,128)}, f32[16,5,16,128]{3,2,1,0:T(8,128)S(1)}, u32[]{:S(2)}, u32[]{:S(2)}) collective-permute-start(f32[16,5,16,128]{3,2,1,0:T(8,128)} %get-tuple-element.13), channel_id=1, source_target_pairs={{0,16},{16,32},{32,48},{48,64},{64,80},{80,96},{96,112},{1,17},{17... | collective-permute-start | bytes 1966088 | tf_op jit(solution)/shard_map/ppermute | solution.py:410
  17.2 3.9 %collective-permute-start.5 = (f32[16,5,16,128]{3,2,1,0:T(8,128)}, f32[16,5,16,128]{3,2,1,0:T(8,128)}, u32[]{:S(2)}, u32[]{:S(2)}) collective-permute-start(f32[16,5,16,128]{3,2,1,0:T(8,128)} %get-tuple-element.14), channel_id=1, source_target_pairs={{16,0},{32,16},{48,32},{64,48},{80,64},{96,80},{112,96},{17,1},{33... | collective-permute-start | bytes 1966088 | tf_op jit(solution)/shard_map/ppermute | solution.py:411
  21.1 0.0 collective-permute-done
  21.2 0.8 broadcast_in_dim.6
  21.9 3.5 %all-to-all-start = ((f32[8,2,16,320]{3,2,1,0:T(8,128)}), f32[8,2,16,320]{3,2,1,0:T(8,128)S(1)}, u32[]{:S(2)}, u32[]{:S(2)}) async-start(f32[8,2,16,320]{3,2,1,0:T(8,128)} %broadcast_in_dim.6), calls=%async_computation | async-start | bytes 786432 | tf_op jit(solution)/shard_map/all_to_all | solution.py:408
  25.4 1.9 %collective-permute-start.3 = (f32[13,5,16,128]{3,2,1,0:T(8,128)}, f32[13,5,16,128]{3,2,1,0:T(8,128)}, u32[]{:S(2)}, u32[]{:S(2)}) collective-permute-start(f32[13,5,16,128]{3,2,1,0:T(8,128)} %get-tuple-element.11), channel_id=1, source_target_pairs={{16,0},{32,16},{48,32},{64,48},{80,64},{96,80},{112,96},{17,1},{33... | collective-permute-start | bytes 1597448 | tf_op jit(solution)/shard_map/ppermute | solution.py:404
  27.3 17.9 %all-to-all-done.mine_ref = f32[8,2,16,320]{3,2,1,0:T(8,128)S(1)} async-done(((f32[8,2,16,320]{3,2,1,0:T(8,128)}), f32[8,2,16,320]{3,2,1,0:T(8,128)S(1)}, u32[]{:S(2)}, u32[]{:S(2)}) %all-to-all-start) | async-done | bytes 327712 | tf_op jit(solution)/shard_map/all_to_all | solution.py:408
  45.2 0.0 collective-permute-start.1
  45.2 0.1 pad_add_fusion.where_ref
  45.3 9.3 %collective-permute-done.3.dn_ref = f32[13,5,16,128]{3,2,1,0:T(8,128)} collective-permute-done((f32[13,5,16,128]{3,2,1,0:T(8,128)}, f32[13,5,16,128]{3,2,1,0:T(8,128)}, u32[]{:S(2)}, u32[]{:S(2)}) %collective-permute-start.3) | collective-permute-done | bytes 532512 | tf_op jit(solution)/shard_map/ppermute | solution.py:404
  54.6 0.0 collective-permute-done.2.up_ref
  54.6 0.0 collective-permute-done.1.other_ref
  54.6 9.0 %adjoint.1 = (f32[6,3,40,16,384]{4,3,2,1,0:T(8,128)S(1)}, f32[40,16,384]{2,1,0:T(8,128)S(1)}) custom-call(s32[2]{0:T(128)S(1)} %pad_add_fusion.where_ref, f32[8,2,16,320]{3,2,1,0:T(8,128)S(1)} %all-to-all-done.mine_ref, f32[8,2,16,320]{3,2,1,0:T(8,128)} %collective-permute-done.1.other_ref, f32[1,3,16,16,320]{4,3,2,1,0:T(8,128)S(1)} %copy-done.2, ...), custom_call_target="tpu_custom_call" | custom-call | tf_op jit(solution)/shard_map/adjoint/pallas_call | solution.py:358
  63.6 0.0 collective-permute-done.5.dn_ref
  63.7 11.1 %forward.1 = (f32[1,3,16,16,320]{4,3,2,1,0:T(8,128)}, f32[16,16,384]{2,1,0:T(8,128)S(1)}) custom-call(s32[2]{0:T(128)S(1)} %pad_add_fusion.where_ref, f32[40,16,384]{2,1,0:T(8,128)S(1)} %get-tuple-element.12.ci_ref, f32[1,3,16,16,320]{4,3,2,1,0:T(8,128)S(1)} %copy-done, f32[1,3,16,16,320]{4,3,2,1,0:T(8,128)S(1)} %copy-done.1, ...), custom_call_target="tpu_custom_call" | custom-call | tf_op jit(solution)/shard_map/forward/pallas_call | solution.py:375
  74.7 13.2 %all_to_all.10 = f32[16,16,384]{2,1,0:T(8,128)S(1)} all-to-all(f32[16,16,384]{2,1,0:T(8,128)S(1)} %get-tuple-element.17), channel_id=1, replica_groups=mesh['tile'=8,'src'=16] {'src'}, dimensions={0} | all-to-all | bytes 786432 | tf_op jit(solution)/shard_map/all_to_all | solution.py:415
  88.0 0.6 fusion
  (10 shorter events, 0.1 us)
Async XLA Ops:
  0.6 20.5 %collective-permute-start = (f32[1,16,320]{2,1,0:T(8,128)}, f32[1,16,320]{2,1,0:T(8,128)S(1)}, u32[]{:S(2)}, u32[]{:S(2)}) collective-permute-start(f32[1,16,320]{2,1,0:T(8,128)} %param.5), channel_id=1, source_target_pairs={{16,0},{17,1},{18,2},{19,3},{20,4},{32,16},{33,17},{34,18},{35,19}... | collective-permute-start | bytes 61448 | tf_op jit(solution)/shard_map/ppermute | solution.py:401
  5.3 15.8 %copy-start.4 = (f32[1,16,320]{2,1,0:T(8,128)S(1)}, f32[1,16,320]{2,1,0:T(8,128)}, u32[]{:S(2)}) copy-start(f32[1,16,320]{2,1,0:T(8,128)} %param.5) | copy-start | bytes 61444
  5.3 49.2 %collective-permute-start.2 = (f32[15,5,16,128]{3,2,1,0:T(8,128)}, f32[15,5,16,128]{3,2,1,0:T(8,128)}, u32[]{:S(2)}, u32[]{:S(2)}) collective-permute-start(f32[15,5,16,128]{3,2,1,0:T(8,128)} %get-tuple-element.10), channel_id=1, source_target_pairs={{0,16},{16,32},{32,48},{48,64},{64,80},{80,96},{96,112},{1,17},{17... | collective-permute-start | bytes 1843208 | tf_op jit(solution)/shard_map/ppermute | solution.py:403
  12.5 42.1 %copy-start.3 = (f32[1,3,16,16,320]{4,3,2,1,0:T(8,128)S(1)}, f32[1,3,16,16,320]{4,3,2,1,0:T(8,128)}, u32[]{:S(2)}) copy-start(f32[1,3,16,16,320]{4,3,2,1,0:T(8,128)} %b_ref.1) | copy-start | bytes 2949124
  15.1 39.4 %copy-start.2 = (f32[1,3,16,16,320]{4,3,2,1,0:T(8,128)S(1)}, f32[1,3,16,16,320]{4,3,2,1,0:T(8,128)}, u32[]{:S(2)}) copy-start(f32[1,3,16,16,320]{4,3,2,1,0:T(8,128)} %a_ref.1) | copy-start | bytes 2949124
  15.1 48.5 %collective-permute-start.4 = (f32[16,5,16,128]{3,2,1,0:T(8,128)}, f32[16,5,16,128]{3,2,1,0:T(8,128)S(1)}, u32[]{:S(2)}, u32[]{:S(2)}) collective-permute-start(f32[16,5,16,128]{3,2,1,0:T(8,128)} %get-tuple-element.13), channel_id=1, source_target_pairs={{0,16},{16,32},{32,48},{48,64},{64,80},{80,96},{96,112},{1,17},{17... | collective-permute-start | bytes 1966088 | tf_op jit(solution)/shard_map/ppermute | solution.py:410
  17.2 46.4 %collective-permute-start.5 = (f32[16,5,16,128]{3,2,1,0:T(8,128)}, f32[16,5,16,128]{3,2,1,0:T(8,128)}, u32[]{:S(2)}, u32[]{:S(2)}) collective-permute-start(f32[16,5,16,128]{3,2,1,0:T(8,128)} %get-tuple-element.14), channel_id=1, source_target_pairs={{16,0},{32,16},{48,32},{64,48},{80,64},{96,80},{112,96},{17,1},{33... | collective-permute-start | bytes 1966088 | tf_op jit(solution)/shard_map/ppermute | solution.py:411
  21.9 23.3 %all-to-all-start = ((f32[8,2,16,320]{3,2,1,0:T(8,128)}), f32[8,2,16,320]{3,2,1,0:T(8,128)S(1)}, u32[]{:S(2)}, u32[]{:S(2)}) async-start(f32[8,2,16,320]{3,2,1,0:T(8,128)} %broadcast_in_dim.6), calls=%async_computation | async-start | bytes 786432 | tf_op jit(solution)/shard_map/all_to_all | solution.py:408
  25.4 29.2 %collective-permute-start.3 = (f32[13,5,16,128]{3,2,1,0:T(8,128)}, f32[13,5,16,128]{3,2,1,0:T(8,128)}, u32[]{:S(2)}, u32[]{:S(2)}) collective-permute-start(f32[13,5,16,128]{3,2,1,0:T(8,128)} %get-tuple-element.11), channel_id=1, source_target_pairs={{16,0},{32,16},{48,32},{64,48},{80,64},{96,80},{112,96},{17,1},{33... | collective-permute-start | bytes 1597448 | tf_op jit(solution)/shard_map/ppermute | solution.py:404
  45.2 9.4 %collective-permute-start.1 = (f32[8,2,16,320]{3,2,1,0:T(8,128)S(1)}, f32[8,2,16,320]{3,2,1,0:T(8,128)}, u32[]{:S(2)}, u32[]{:S(2)}) collective-permute-start(f32[8,2,16,320]{3,2,1,0:T(8,128)S(1)} %all-to-all-done.mine_ref), channel_id=1, source_target_pairs={{0,1},{1,0},{2,3},{3,2},{4,5},{5,4},{6,7},{7,6},{8,9},{9,8},{10,11... | collective-permute-start | bytes 983048 | tf_op jit(solution)/shard_map/ppermute | solution.py:412
  45.3 18.4 %copy-start = (f32[1,3,16,16,320]{4,3,2,1,0:T(8,128)S(1)}, f32[1,3,16,16,320]{4,3,2,1,0:T(8,128)}, u32[]{:S(2)}) copy-start(f32[1,3,16,16,320]{4,3,2,1,0:T(8,128)} %e0_ref.1) | copy-start | bytes 2949124
  45.3 18.4 %copy-start.1 = (f32[1,3,16,16,320]{4,3,2,1,0:T(8,128)S(1)}, f32[1,3,16,16,320]{4,3,2,1,0:T(8,128)}, u32[]{:S(2)}) copy-start(f32[1,3,16,16,320]{4,3,2,1,0:T(8,128)} %h0_ref.1) | copy-start | bytes 2949124

commit v4 on v3

--- a/solution.py
+++ b/solution.py
@@ -37,53 +37,60 @@
     return h(2, p) - courant * ((e(1, p + 1) - e(1, p)) - ahead)
 
 
-def pack_body(depth, e_hbm, h_hbm, up_ref, dn_ref, low_ref, high_ref, sem):
-    def edges(upward):
-        start, ref = (NX - depth, high_ref) if upward else (0, low_ref)
-        return [
-            pltpu.make_async_copy(x.at[0, :, pl.ds(start, depth)], ref.at[a], sem.at[2 * upward + a])
-            for a, x in enumerate((e_hbm, h_hbm))
+def pack_body(a_hbm, b_hbm, e_hbm, h_hbm, *refs):
+    outs, edges, packed, sem = refs[:4], refs[4:8], refs[8:12], refs[12]
+    work = []
+    for k, (depth, upward) in enumerate(HALOS):
+        start = NX - depth if upward else 0
+        fields = (e_hbm, h_hbm) if depth == STEPS else (a_hbm, b_hbm)
+        copies = [
+            pltpu.make_async_copy(x.at[0, :, pl.ds(start, depth)], edges[k].at[j], sem.at[k, j]) for j, x in enumerate(fields)
         ]
-
-    copies = {upward: edges(upward) for upward in (True, False)}
-    for upward in (True, False):
-        for copy in copies[upward]:
+        for copy in copies:
             copy.start()
-    for upward, out in ((True, up_ref), (False, dn_ref)):
-        for copy in copies[upward]:
+        work.append((start, copies))
+    leaving = []
+    for k, (depth, upward) in enumerate(HALOS):
+        start, copies = work[k]
+        for copy in copies:
             copy.wait()
-        ref, base = (high_ref, NX - depth) if upward else (low_ref, 0)
-        at = lambda a: lambda c, p, a=a, ref=ref, base=base: ref[a, c, p - base]
+        at = lambda a: lambda c, p, a=a, ref=edges[k], start=start: ref[a, c, p - start]
         planes = plane_list(depth, upward)
-        for k in range(len(planes) // 2):
+        out = packed[k]
+        for i in range(len(planes) // 2):
             tails = []
             for j in range(2):
-                a, c, p = planes[2 * k + j]
+                a, c, p = planes[2 * i + j]
                 x = first_half_step(at(0), at(1), NX - depth, c) if a == 2 else at(a)(c, p)
-                out[k, 2 * j] = x[:, 0:128]
-                out[k, 2 * j + 1] = x[:, 128:256]
+                out[i, 2 * j] = x[:, 0:128]
+                out[i, 2 * j + 1] = x[:, 128:256]
                 tails.append(x[:, 256:320])
-            out[k, 4] = jnp.concatenate(tails, axis=1)
-
-
-def pack(depth, e, h):
-    up = len(plane_list(depth, True)) // 2
-    dn = len(plane_list(depth, False)) // 2
+            out[i, 4] = jnp.concatenate(tails, axis=1)
+        copy = pltpu.make_async_copy(out, outs[k], sem.at[k, 2])
+        copy.start()
+        leaving.append(copy)
+    for copy in leaving:
+        copy.wait()
+
+
+HALOS = ((STEPS - 1, True), (STEPS - 1, False), (STEPS, True), (STEPS, False))
+
+
+def pack(*fields):
+    sizes = [(len(plane_list(depth, upward)) // 2, 5, 16, 128) for depth, upward in HALOS]
     return pl.pallas_call(
-        lambda *refs: pack_body(depth, *refs),
-        out_shape=(
-            jax.ShapeDtypeStruct((up, 5, 16, 128), F32),
-            jax.ShapeDtypeStruct((dn, 5, 16, 128), F32),
-        ),
-        in_specs=[HBM] * 2,
-        out_specs=[pl.BlockSpec(memory_space=pltpu.VMEM)] * 2,
+        pack_body,
+        out_shape=[jax.ShapeDtypeStruct(size, F32) for size in sizes],
+        in_specs=[HBM] * 4,
+        out_specs=[HBM] * 4,
         scratch_shapes=[
-            pltpu.VMEM((2, 3, depth, NY, NZ), F32),
-            pltpu.VMEM((2, 3, depth, NY, NZ), F32),
-            pltpu.SemaphoreType.DMA((4,)),
+            *(pltpu.VMEM((2, 3, depth, NY, NZ), F32) for depth, _ in HALOS),
+            *(pltpu.VMEM(size, F32) for size in sizes),
+            pltpu.SemaphoreType.DMA((4, 3)),
         ],
         compiler_params=pltpu.CompilerParams(vmem_limit_bytes=60 << 20),
-    )(e, h)
+        name="pack",
+    )(*fields)
 
 
 def unpack(depth, buf, upward, put):
@@ -399,14 +406,13 @@
     near += [(t * sources + s, (t + 1) * sources + s) for t in range(tiles - 1) for s in range(NX - DEEP + 1, NX)]
 
     border = lax.ppermute(permittivity, ("tile", "src"), near)
-    a_up, a_dn = pack(STEPS - 1, e_cotangent, h_cotangent)
+    a_up, a_dn, e_up, e_dn = pack(e_cotangent, h_cotangent, e_start, h_start)
     a_up = lax.ppermute(a_up, "tile", upward)
     a_dn = lax.ppermute(a_dn, "tile", downward)
     both = jnp.concatenate([permittivity, border], axis=0)
     groups = [list(range(k, sources, 2)) for k in range(2)]
     both = jnp.broadcast_to(both, (sources // 2, *both.shape))
     mine = lax.all_to_all(both, "src", 0, 0, tiled=True, axis_index_groups=groups)
-    e_up, e_dn = pack(STEPS, e_start, h_start)
     e_up = lax.ppermute(e_up, "tile", upward)
     e_dn = lax.ppermute(e_dn, "tile", downward)
     other = lax.ppermute(mine, "src", [(s, s ^ 1) for s in range(sources)])

time: 89.1 us -> 87.1 us (0.978)
  Pallas kernels: 25.1 us -> 23.1 us
    ppermute x1, waiting for transfers between devices: 9.26 us -> 6.49 us  [on_device(): a_dn = lax.ppermute(a_dn, 'tile', downward)]
    all_to_all x1, waiting for transfers between devices: 17.9 us -> 20.7 us  [on_device(): lax.all_to_all(both, 'src', 0, 0, tiled=True, axis_index_groups=groups)]
    pallas_call x2 -> x1, Pallas kernels: 4.98 us -> 3.01 us  [pack(): pl.pallas_call(pack_body, out_shape=[jax.ShapeDtypeStruct(size, F32) for...]
  transfers between devices with their start and end apart: 7 -> 7, of which waited for: 2 -> 2; matrix products, arithmetic and copies ran while one was open for 1% -> 1% of each run, Pallas kernels for 16% -> 14%
where the time goes in v4:
time: 87.1 us; the launch traced here: 86.6 us
  waiting for transfers between devices  27.2 us (31%)
  Pallas kernels  23.1 us (27%)
  starting transfers between devices  20.8 us (24%)
  blocking collectives  13.2 us (15%)
    all_to_all x1, waiting for transfers between devices, on_device(): lax.all_to_all(both, 'src', 0, 0, tiled=True, axis_index_groups=groups)  20.7 us
    all_to_all x1, blocking collectives, on_device(): parts = lax.all_to_all(sums, 'src', 0, 0, tiled=True)  13.2 us
    pallas_call x1, Pallas kernels, forward(): pl.pallas_call(forward_body, out_shape=(shape(1, 3, NX, NY, NZ), shape(NX...  11.1 us
    pallas_call x1, Pallas kernels, adjoint(): pl.pallas_call(adjoint_body, out_shape=(shape(STEPS, *FIELD), shape(ALL,...  9.04 us
    ppermute x1, starting transfers between devices, on_device(): a_up = lax.ppermute(a_up, 'tile', upward)  7.28 us
    ppermute x1, waiting for transfers between devices, on_device(): a_dn = lax.ppermute(a_dn, 'tile', downward)  6.49 us
    ppermute x1, starting transfers between devices, on_device(): e_dn = lax.ppermute(e_dn, 'tile', downward)  3.92 us
    all_to_all x1, starting transfers between devices, on_device(): lax.all_to_all(both, 'src', 0, 0, tiled=True, axis_index_groups=groups)  3.45 us
  transfers between devices with their start and end apart: 7, of which 2 were waited for; matrix products, arithmetic and copies ran while one was open for 1% of the time, Pallas kernels for 14%

profile of v4, /device:TPU:96, one launch (start us, length us, event | category | flops | bytes accessed | tf_op | source)
XLA Modules:
  0.0 86.6 jit_solution(5108739817473535991)
XLA Ops:
  0.6 2.3 %collective-permute-start = (f32[1,16,320]{2,1,0:T(8,128)}, f32[1,16,320]{2,1,0:T(8,128)S(1)}, u32[]{:S(2)}, u32[]{:S(2)}) collective-permute-start(f32[1,16,320]{2,1,0:T(8,128)} %param.5), channel_id=1, source_target_pairs={{16,0},{17,1},{18,2},{19,3},{20,4},{32,16},{33,17},{34,18},{35,19}... | collective-permute-start | bytes 61448 | tf_op jit(solution)/shard_map/ppermute | solution.py:408
  3.0 0.0 copy-start.3
  3.0 3.0 %pack.1 = (f32[15,5,16,128]{3,2,1,0:T(8,128)}, f32[13,5,16,128]{3,2,1,0:T(8,128)}, f32[16,5,16,128]{3,2,1,0:T(8,128)}, f32[16,5,16,128]{3,2,1,0:T(8,128)}) custom-call(f32[1,3,16,16,320]{4,3,2,1,0:T(8,128)} %a_ref.1, f32[1,3,16,16,320]{4,3,2,1,0:T(8,128)} %b_ref.1, f32[1,3,16,16,320]{4,3,2,1,0:T(8,128)} %e0_ref.1, f32[1,3,16,16,320]{4,3,2,1,0:T(8,128)} %h0_ref.1), custom_call_target="tpu_custom_call" | custom-call | tf_op jit(solution)/shard_map/pack/pallas_call | solution.py:81
  6.0 0.0 copy-start.2
  6.0 7.3 %collective-permute-start.2 = (f32[15,5,16,128]{3,2,1,0:T(8,128)}, f32[15,5,16,128]{3,2,1,0:T(8,128)}, u32[]{:S(2)}, u32[]{:S(2)}) collective-permute-start(f32[15,5,16,128]{3,2,1,0:T(8,128)} %get-tuple-element.10), channel_id=1, source_target_pairs={{0,16},{16,32},{32,48},{48,64},{64,80},{80,96},{96,112},{1,17},{17... | collective-permute-start | bytes 1843208 | tf_op jit(solution)/shard_map/ppermute | solution.py:410
  13.3 1.9 %collective-permute-start.4 = (f32[16,5,16,128]{3,2,1,0:T(8,128)}, f32[16,5,16,128]{3,2,1,0:T(8,128)S(1)}, u32[]{:S(2)}, u32[]{:S(2)}) collective-permute-start(f32[16,5,16,128]{3,2,1,0:T(8,128)} %get-tuple-element.13), channel_id=1, source_target_pairs={{0,16},{16,32},{32,48},{48,64},{64,80},{80,96},{96,112},{1,17},{17... | collective-permute-start | bytes 1966088 | tf_op jit(solution)/shard_map/ppermute | solution.py:416
  15.2 3.9 %collective-permute-start.5 = (f32[16,5,16,128]{3,2,1,0:T(8,128)}, f32[16,5,16,128]{3,2,1,0:T(8,128)}, u32[]{:S(2)}, u32[]{:S(2)}) collective-permute-start(f32[16,5,16,128]{3,2,1,0:T(8,128)} %get-tuple-element.14), channel_id=1, source_target_pairs={{16,0},{32,16},{48,32},{64,48},{80,64},{96,80},{112,96},{17,1},{33... | collective-permute-start | bytes 1966088 | tf_op jit(solution)/shard_map/ppermute | solution.py:417
  19.1 0.0 collective-permute-done
  19.2 0.8 broadcast_in_dim.6
  20.0 3.5 %all-to-all-start = ((f32[8,2,16,320]{3,2,1,0:T(8,128)}), f32[8,2,16,320]{3,2,1,0:T(8,128)S(1)}, u32[]{:S(2)}, u32[]{:S(2)}) async-start(f32[8,2,16,320]{3,2,1,0:T(8,128)} %broadcast_in_dim.6), calls=%async_computation | async-start | bytes 786432 | tf_op jit(solution)/shard_map/all_to_all | solution.py:415
  23.4 1.9 %collective-permute-start.3 = (f32[13,5,16,128]{3,2,1,0:T(8,128)}, f32[13,5,16,128]{3,2,1,0:T(8,128)}, u32[]{:S(2)}, u32[]{:S(2)}) collective-permute-start(f32[13,5,16,128]{3,2,1,0:T(8,128)} %get-tuple-element.11), channel_id=1, source_target_pairs={{16,0},{32,16},{48,32},{64,48},{80,64},{96,80},{112,96},{17,1},{33... | collective-permute-start | bytes 1597448 | tf_op jit(solution)/shard_map/ppermute | solution.py:411
  25.3 20.7 %all-to-all-done.mine_ref = f32[8,2,16,320]{3,2,1,0:T(8,128)S(1)} async-done(((f32[8,2,16,320]{3,2,1,0:T(8,128)}), f32[8,2,16,320]{3,2,1,0:T(8,128)S(1)}, u32[]{:S(2)}, u32[]{:S(2)}) %all-to-all-start) | async-done | bytes 327712 | tf_op jit(solution)/shard_map/all_to_all | solution.py:415
  46.0 0.0 collective-permute-start.1
  46.0 0.1 pad_add_fusion.where_ref
  46.1 6.5 %collective-permute-done.3.dn_ref = f32[13,5,16,128]{3,2,1,0:T(8,128)} collective-permute-done((f32[13,5,16,128]{3,2,1,0:T(8,128)}, f32[13,5,16,128]{3,2,1,0:T(8,128)}, u32[]{:S(2)}, u32[]{:S(2)}) %collective-permute-start.3) | collective-permute-done | bytes 532512 | tf_op jit(solution)/shard_map/ppermute | solution.py:411
  52.6 0.0 collective-permute-done.2.up_ref
  52.6 0.0 collective-permute-done.1.other_ref
  52.6 0.0 copy-done.2
  52.6 9.0 %adjoint.1 = (f32[6,3,40,16,384]{4,3,2,1,0:T(8,128)S(1)}, f32[40,16,384]{2,1,0:T(8,128)S(1)}) custom-call(s32[2]{0:T(128)S(1)} %pad_add_fusion.where_ref, f32[8,2,16,320]{3,2,1,0:T(8,128)S(1)} %all-to-all-done.mine_ref, f32[8,2,16,320]{3,2,1,0:T(8,128)} %collective-permute-done.1.other_ref, f32[1,3,16,16,320]{4,3,2,1,0:T(8,128)S(1)} %copy-done.2, ...), custom_call_target="tpu_custom_call" | custom-call | tf_op jit(solution)/shard_map/adjoint/pallas_call | solution.py:365
  61.6 0.0 collective-permute-done.4.up_ref
  61.7 0.0 collective-permute-done.5.dn_ref
  61.7 11.1 %forward.1 = (f32[1,3,16,16,320]{4,3,2,1,0:T(8,128)}, f32[16,16,384]{2,1,0:T(8,128)S(1)}) custom-call(s32[2]{0:T(128)S(1)} %pad_add_fusion.where_ref, f32[40,16,384]{2,1,0:T(8,128)S(1)} %get-tuple-element.12.ci_ref, f32[1,3,16,16,320]{4,3,2,1,0:T(8,128)S(1)} %copy-done, f32[1,3,16,16,320]{4,3,2,1,0:T(8,128)S(1)} %copy-done.1, ...), custom_call_target="tpu_custom_call" | custom-call | tf_op jit(solution)/shard_map/forward/pallas_call | solution.py:382
  72.7 13.2 %all_to_all.10 = f32[16,16,384]{2,1,0:T(8,128)S(1)} all-to-all(f32[16,16,384]{2,1,0:T(8,128)S(1)} %get-tuple-element.17), channel_id=1, replica_groups=mesh['tile'=8,'src'=16] {'src'}, dimensions={0} | all-to-all | bytes 786432 | tf_op jit(solution)/shard_map/all_to_all | solution.py:421
  86.0 0.6 fusion
  (9 shorter events, 0.0 us)
Async XLA Ops:
  0.6 18.5 %copy-start.4 = (f32[1,16,320]{2,1,0:T(8,128)S(1)}, f32[1,16,320]{2,1,0:T(8,128)}, u32[]{:S(2)}) copy-start(f32[1,16,320]{2,1,0:T(8,128)} %param.5) | copy-start | bytes 61444
  0.6 18.5 %collective-permute-start = (f32[1,16,320]{2,1,0:T(8,128)}, f32[1,16,320]{2,1,0:T(8,128)S(1)}, u32[]{:S(2)}, u32[]{:S(2)}) collective-permute-start(f32[1,16,320]{2,1,0:T(8,128)} %param.5), channel_id=1, source_target_pairs={{16,0},{17,1},{18,2},{19,3},{20,4},{32,16},{33,17},{34,18},{35,19}... | collective-permute-start | bytes 61448 | tf_op jit(solution)/shard_map/ppermute | solution.py:408
  3.0 49.6 %copy-start.3 = (f32[1,3,16,16,320]{4,3,2,1,0:T(8,128)S(1)}, f32[1,3,16,16,320]{4,3,2,1,0:T(8,128)}, u32[]{:S(2)}) copy-start(f32[1,3,16,16,320]{4,3,2,1,0:T(8,128)} %b_ref.1) | copy-start | bytes 2949124
  6.0 46.6 %copy-start.2 = (f32[1,3,16,16,320]{4,3,2,1,0:T(8,128)S(1)}, f32[1,3,16,16,320]{4,3,2,1,0:T(8,128)}, u32[]{:S(2)}) copy-start(f32[1,3,16,16,320]{4,3,2,1,0:T(8,128)} %a_ref.1) | copy-start | bytes 2949124
  6.0 46.6 %collective-permute-start.2 = (f32[15,5,16,128]{3,2,1,0:T(8,128)}, f32[15,5,16,128]{3,2,1,0:T(8,128)}, u32[]{:S(2)}, u32[]{:S(2)}) collective-permute-start(f32[15,5,16,128]{3,2,1,0:T(8,128)} %get-tuple-element.10), channel_id=1, source_target_pairs={{0,16},{16,32},{32,48},{48,64},{64,80},{80,96},{96,112},{1,17},{17... | collective-permute-start | bytes 1843208 | tf_op jit(solution)/shard_map/ppermute | solution.py:410
  13.3 48.4 %collective-permute-start.4 = (f32[16,5,16,128]{3,2,1,0:T(8,128)}, f32[16,5,16,128]{3,2,1,0:T(8,128)S(1)}, u32[]{:S(2)}, u32[]{:S(2)}) collective-permute-start(f32[16,5,16,128]{3,2,1,0:T(8,128)} %get-tuple-element.13), channel_id=1, source_target_pairs={{0,16},{16,32},{32,48},{48,64},{64,80},{80,96},{96,112},{1,17},{17... | collective-permute-start | bytes 1966088 | tf_op jit(solution)/shard_map/ppermute | solution.py:416
  15.2 46.4 %collective-permute-start.5 = (f32[16,5,16,128]{3,2,1,0:T(8,128)}, f32[16,5,16,128]{3,2,1,0:T(8,128)}, u32[]{:S(2)}, u32[]{:S(2)}) collective-permute-start(f32[16,5,16,128]{3,2,1,0:T(8,128)} %get-tuple-element.14), channel_id=1, source_target_pairs={{16,0},{32,16},{48,32},{64,48},{80,64},{96,80},{112,96},{17,1},{33... | collective-permute-start | bytes 1966088 | tf_op jit(solution)/shard_map/ppermute | solution.py:417
  20.0 26.0 %all-to-all-start = ((f32[8,2,16,320]{3,2,1,0:T(8,128)}), f32[8,2,16,320]{3,2,1,0:T(8,128)S(1)}, u32[]{:S(2)}, u32[]{:S(2)}) async-start(f32[8,2,16,320]{3,2,1,0:T(8,128)} %broadcast_in_dim.6), calls=%async_computation | async-start | bytes 786432 | tf_op jit(solution)/shard_map/all_to_all | solution.py:415
  23.4 29.2 %collective-permute-start.3 = (f32[13,5,16,128]{3,2,1,0:T(8,128)}, f32[13,5,16,128]{3,2,1,0:T(8,128)}, u32[]{:S(2)}, u32[]{:S(2)}) collective-permute-start(f32[13,5,16,128]{3,2,1,0:T(8,128)} %get-tuple-element.11), channel_id=1, source_target_pairs={{16,0},{32,16},{48,32},{64,48},{80,64},{96,80},{112,96},{17,1},{33... | collective-permute-start | bytes 1597448 | tf_op jit(solution)/shard_map/ppermute | solution.py:411
  46.0 6.6 %collective-permute-start.1 = (f32[8,2,16,320]{3,2,1,0:T(8,128)S(1)}, f32[8,2,16,320]{3,2,1,0:T(8,128)}, u32[]{:S(2)}, u32[]{:S(2)}) collective-permute-start(f32[8,2,16,320]{3,2,1,0:T(8,128)S(1)} %all-to-all-done.mine_ref), channel_id=1, source_target_pairs={{0,1},{1,0},{2,3},{3,2},{4,5},{5,4},{6,7},{7,6},{8,9},{9,8},{10,11... | collective-permute-start | bytes 983048 | tf_op jit(solution)/shard_map/ppermute | solution.py:418
  46.1 15.6 %copy-start = (f32[1,3,16,16,320]{4,3,2,1,0:T(8,128)S(1)}, f32[1,3,16,16,320]{4,3,2,1,0:T(8,128)}, u32[]{:S(2)}) copy-start(f32[1,3,16,16,320]{4,3,2,1,0:T(8,128)} %e0_ref.1) | copy-start | bytes 2949124
  46.1 15.6 %copy-start.1 = (f32[1,3,16,16,320]{4,3,2,1,0:T(8,128)S(1)}, f32[1,3,16,16,320]{4,3,2,1,0:T(8,128)}, u32[]{:S(2)}) copy-start(f32[1,3,16,16,320]{4,3,2,1,0:T(8,128)} %h0_ref.1) | copy-start | bytes 2949124
